TPU v7x, 32 devices: a whole 2x2x4 slice. The times are simulated.
32 devices in a mesh: grp: 2 (over y), slab: 8 (over z, x), col: 2 (over core).
Axes of the slice: x: 2, y: 2, z: 4, core: 2. Of those that a mesh axis runs over, the one named last changes fastest.
Arguments:
- states: float32 [4, 64, 128, 1024], P(None, ('grp', 'slab'), 'col'), parts along dimension 1, may hold values from 0 to 1.4, as said below
- cond: float32 [6, 16, 32, 256], P(None, ('grp', 'slab'), 'col'), parts along dimension 1, may hold values from -0.025 to 0.15, as said below
- tension: float32 [32, 64, 512], P(('grp', 'slab'), 'col'), parts along dimension 0, may hold values from 0 to 1
- fiber: int32 [16, 32, 256], P(('grp', 'slab'), 'col'), parts along dimension 0, may hold values from 0 to 63
- disp: float32 [3, 16, 32, 256], P(None, ('grp', 'slab'), 'col'), parts along dimension 1, may hold values from -0.12 to 0.12
Outputs:
- states_next: float32 [4, 64, 128, 1024], P(None, ('grp', 'slab'), 'col'), parts along dimension 1
- tension_next: float32 [32, 64, 512], P(('grp', 'slab'), 'col'), parts along dimension 0
- disp_next: float32 [3, 16, 32, 256], P(None, ('grp', 'slab'), 'col'), parts along dimension 1
- cond_next: float32 [6, 16, 32, 256], P(None, ('grp', 'slab'), 'col'), parts along dimension 1
There are 2 independent parts, one for each index of `grp`. A program takes and returns all parts, laid end to end along the dimension named above; each array names one. Nothing has to cross between parts.
Inputs may be any that keep to these rules, and one draw needn't show every extreme that they name: `states`: component 0 lies in 0 to 1.4, components 1 to 3 in 0 to 1. `cond`: components 0 to 2 lie in 0.05 to 0.15, components 3 to 5 in -0.025 to 0.025.
All inputs are finite; a program needn't handle non-finite values.
Results may differ from a plain program's by a relative error of at most 0.0003.
Values sent between devices are 32-bit elements; how exact they have to be, the bound alone decides.
A program may use at most 192 MiB of HBM per device.

v0:
```python
import jax
import jax.numpy as jnp
from jax import lax
from jax.sharding import PartitionSpec as P

SUB = 4
MECH_STEPS = 2
NFIB = 64


SHARP = 50.0
STEP_TIME = 0.05
LAME_FIRST = 1.0
SHEAR = 0.5
ACTIVE_GAIN = 0.5
MECH_RATE = 0.15
SIGMA_LONG = 0.16
SIGMA_TRANS = 0.04
SMOOTH_WEIGHTS = (0.125, 0.75, 0.125)
SLOPE_WEIGHTS = (-0.5, 0.0, 0.5)
PAIRS = ((0, 0), (1, 1), (2, 2), (0, 1), (0, 2), (1, 2))


def extended(array, sides, width):
    for axis, dim in sides:
        devices, length = (lax.axis_size(axis), array.shape[dim])
        up = [(i, (i + 1) % devices) for i in range(devices - 1)]
        down = [(j, i) for i, j in up]
        last = lax.slice_in_dim(array, length - width, length, axis=dim)
        initial = lax.slice_in_dim(array, 0, width, axis=dim)
        before = lax.ppermute(last, axis, up)
        after = lax.ppermute(initial, axis, down)
        array = jnp.concatenate([before, array, after], axis=dim)
    return array


def switch(value):
    return 0.5 * (1.0 + jnp.tanh(SHARP * value))


def ionic_rates(volt, gate_v, gate_w, gate_s):
    high_v = switch(volt - 0.3)
    high_w = switch(volt - 0.13)
    high_o = switch(volt - 0.006)
    tau_vminus = (1.0 - high_o) * 60.0 + high_o * 1150.0
    tau_wminus = 60.0 + (15.0 - 60.0) * 0.5 * (1.0 + jnp.tanh(65.0 * (volt - 0.03)))
    tau_soft = 30.0181 + (0.9957 - 30.0181) * 0.5 * (1.0 + jnp.tanh(2.0458 * (volt - 0.65)))
    tau_slow = (1.0 - high_w) * 2.7342 + high_w * 16.0
    tau_open = (1.0 - high_o) * 400.0 + high_o * 6.0
    v_inf = 1.0 - high_o
    w_inf = (1.0 - high_o) * (1.0 - volt / 0.07) + high_o * 0.94
    fast_current = -gate_v * high_v * (volt - 0.3) * (1.55 - volt) / 0.11
    outward = volt * (1.0 - high_w) / tau_open + high_w / tau_soft
    slow_current = -high_w * gate_w * gate_s / 1.8875
    rate_v = (1.0 - high_v) * (v_inf - gate_v) / tau_vminus - high_v * gate_v / 1.4506
    rate_w = (1.0 - high_w) * (w_inf - gate_w) / tau_wminus - high_w * gate_w / 200.0
    rate_s = (0.5 * (1.0 + jnp.tanh(2.0994 * (volt - 0.9087))) - gate_s) / tau_slow
    return (-(fast_current + outward + slow_current), rate_v, rate_w, rate_s)


def diffusion(padded, coeff):
    centre = padded[1:-1, 1:-1, 1:-1]
    along_z = padded[2:, 1:-1, 1:-1] + padded[:-2, 1:-1, 1:-1] - 2.0 * centre
    along_y = padded[1:-1, 2:, 1:-1] + padded[1:-1, :-2, 1:-1] - 2.0 * centre
    along_x = padded[1:-1, 1:-1, 2:] + padded[1:-1, 1:-1, :-2] - 2.0 * centre
    cross_zy = 0.25 * (
        padded[2:, 2:, 1:-1]
        - padded[2:, :-2, 1:-1]
        - padded[:-2, 2:, 1:-1]
        + padded[:-2, :-2, 1:-1]
    )
    cross_zx = 0.25 * (
        padded[2:, 1:-1, 2:]
        - padded[2:, 1:-1, :-2]
        - padded[:-2, 1:-1, 2:]
        + padded[:-2, 1:-1, :-2]
    )
    cross_yx = 0.25 * (
        padded[1:-1, 2:, 2:]
        - padded[1:-1, 2:, :-2]
        - padded[1:-1, :-2, 2:]
        + padded[1:-1, :-2, :-2]
    )
    return (
        coeff[0] * along_z
        + coeff[1] * along_y
        + coeff[2] * along_x
        + 2.0 * (coeff[3] * cross_zy + coeff[4] * cross_zx + coeff[5] * cross_yx)
    )


def excite_step(padded, volt, gate_v, gate_w, gate_s, coeff):
    ion, rate_v, rate_w, rate_s = ionic_rates(volt, gate_v, gate_w, gate_s)
    new_volt = volt + diffusion(padded, coeff) + STEP_TIME * ion
    return (
        new_volt,
        gate_v + STEP_TIME * rate_v,
        gate_w + STEP_TIME * rate_w,
        gate_s + STEP_TIME * rate_s,
    )


def upsample(cond):
    return jnp.repeat(jnp.repeat(jnp.repeat(cond, 4, axis=1), 4, axis=2), 4, axis=3)


def coarsen(field):
    shaped = field.reshape(field.shape[0] // 2, 2, field.shape[1] // 2, 2, field.shape[2] // 2, 2)
    return jnp.mean(shaped, axis=(1, 3, 5))


def fiber_dir(fiber):
    block_index = fiber.astype(jnp.float32)
    theta = -1.0 + 2.0 * block_index / (NFIB - 1)
    tilt = 0.3 * jnp.sin(3.0 * block_index)
    return jnp.stack(
        [jnp.sin(tilt), jnp.cos(tilt) * jnp.sin(theta), jnp.cos(tilt) * jnp.cos(theta)]
    )


def along(field, axis_pos, weights):
    count = field.shape[axis_pos] - 2
    total = weights[0] * lax.slice_in_dim(field, 0, count, axis=axis_pos)
    total = total + weights[1] * lax.slice_in_dim(field, 1, count + 1, axis=axis_pos)
    return total + weights[2] * lax.slice_in_dim(field, 2, count + 2, axis=axis_pos)


def spline_op(padded, direction):
    result = padded
    for dim_pos in range(3):
        result = along(
            result, dim_pos + 1, SLOPE_WEIGHTS if dim_pos == direction else SMOOTH_WEIGHTS
        )
    return result


def deformation(padded_disp):
    grads = [spline_op(padded_disp, direction) for direction in range(3)]
    return [
        [grads[col_pos][row_pos] + (1.0 if row_pos == col_pos else 0.0) for col_pos in range(3)]
        for row_pos in range(3)
    ]


def first_piola(deform, active, fdir):
    right = [
        [
            deform[0][a_pos] * deform[0][b_pos]
            + deform[1][a_pos] * deform[1][b_pos]
            + deform[2][a_pos] * deform[2][b_pos]
            for b_pos in range(3)
        ]
        for a_pos in range(3)
    ]
    strain = [
        [0.5 * (right[a_pos][b_pos] - (1.0 if a_pos == b_pos else 0.0)) for b_pos in range(3)]
        for a_pos in range(3)
    ]
    trace_e = strain[0][0] + strain[1][1] + strain[2][2]
    second = []
    for a_pos in range(3):
        row_list = []
        for b_pos in range(3):
            entry = (
                2.0 * SHEAR * strain[a_pos][b_pos]
                + ACTIVE_GAIN * active * fdir[a_pos] * fdir[b_pos]
            )
            if a_pos == b_pos:
                entry = LAME_FIRST * trace_e + entry
            row_list.append(entry)
        second.append(row_list)
    pieces = []
    for a_pos in range(3):
        for i_pos in range(3):
            pieces.append(
                deform[i_pos][0] * second[0][a_pos]
                + deform[i_pos][1] * second[1][a_pos]
                + deform[i_pos][2] * second[2][a_pos]
            )
    return jnp.stack(pieces)


def forces(padded_piola):
    total = spline_op(padded_piola[0:3], 0)
    total = total + spline_op(padded_piola[3:6], 1)
    return total + spline_op(padded_piola[6:9], 2)


def metric(deform, fdir):
    det_f = (
        deform[0][0] * (deform[1][1] * deform[2][2] - deform[1][2] * deform[2][1])
        - deform[0][1] * (deform[1][0] * deform[2][2] - deform[1][2] * deform[2][0])
        + deform[0][2] * (deform[1][0] * deform[2][1] - deform[1][1] * deform[2][0])
    )
    inverse = [[None, None, None] for row_pos in range(3)]
    for i_pos in range(3):
        for j_pos in range(3):
            cofac = (
                deform[(i_pos + 1) % 3][(j_pos + 1) % 3] * deform[(i_pos + 2) % 3][(j_pos + 2) % 3]
                - deform[(i_pos + 1) % 3][(j_pos + 2) % 3]
                * deform[(i_pos + 2) % 3][(j_pos + 1) % 3]
            )
            inverse[j_pos][i_pos] = cofac / det_f
    along_fiber = [
        inverse[a_pos][0] * fdir[0] + inverse[a_pos][1] * fdir[1] + inverse[a_pos][2] * fdir[2]
        for a_pos in range(3)
    ]
    comps = []
    for a_pos, b_pos in PAIRS:
        inv_metric = (
            inverse[a_pos][0] * inverse[b_pos][0]
            + inverse[a_pos][1] * inverse[b_pos][1]
            + inverse[a_pos][2] * inverse[b_pos][2]
        )
        comps.append(
            SIGMA_TRANS * inv_metric
            + (SIGMA_LONG - SIGMA_TRANS) * along_fiber[a_pos] * along_fiber[b_pos]
        )
    return jnp.stack(comps)


def mechanics(disp, active, fdir, extend):
    for turn_index in range(MECH_STEPS):
        deform = deformation(extend(disp))
        piola = first_piola(deform, active, fdir)
        disp = disp + MECH_RATE * forces(extend(piola))
    deform = deformation(extend(disp))
    return (disp, metric(deform, fdir))


def pad_last(field):
    return jnp.pad(field, [(0, 0)] * (field.ndim - 1) + [(1, 1)])


def extend_spread(field):
    return pad_last(extended(field, (("slab", 1), ("col", 2)), 1))


def on_device(states, cond, tension, fiber, disp):
    volt, gate_v, gate_w, gate_s = (states[0], states[1], states[2], states[3])
    coeff = upsample(cond)
    for turn_index in range(SUB):
        padded = pad_last(extended(volt, (("slab", 0), ("col", 1)), 1))
        volt, gate_v, gate_w, gate_s = excite_step(padded, volt, gate_v, gate_w, gate_s, coeff)
    states_next = jnp.stack([volt, gate_v, gate_w, gate_s])
    tension_next = tension + 0.5 * (coarsen(volt) - tension)
    active = coarsen(tension_next)
    fdir = fiber_dir(fiber)
    disp_next, cond_next = mechanics(disp, active, fdir, extend_spread)
    return (states_next, tension_next, disp_next, cond_next)


def solution(mesh):
    in_specs = (
        P(None, ("grp", "slab"), "col", None),
        P(None, ("grp", "slab"), "col", None),
        P(("grp", "slab"), "col", None),
        P(("grp", "slab"), "col", None),
        P(None, ("grp", "slab"), "col", None),
    )
    out_specs = (
        P(None, ("grp", "slab"), "col", None),
        P(("grp", "slab"), "col", None),
        P(None, ("grp", "slab"), "col", None),
        P(None, ("grp", "slab"), "col", None),
    )
    return jax.shard_map(
        on_device, mesh=mesh, in_specs=in_specs, out_specs=out_specs, check_vma=False
    )
```

profile of v0, /device:TPU:0, one launch (start us, length us, event | category | flops | bytes accessed | tf_op | source)
XLA Modules:
  0.0 313.0 jit_solution(10889490930675842464)
XLA Ops:
  0.6 5.5 %collective-permute-start.16 = (f32[3,1,16,256]{3,2,1,0:T(8,128)}, f32[3,1,16,256]{3,2,1,0:T(8,128)}, u32[]{:S(2)}, u32[]{:S(2)}) collective-permute-start(f32[3,1,16,256]{3,2,1,0:T(8,128)} %param.9), channel_id=1, source_target_pairs={{0,2},{2,4},{4,6},{6,8},{8,10},{10,12},{12,14},{1,3},{3,5},{5,7},{... | collective-permute-start | bytes 147464 | tf_op jit(solution)/shard_map/ppermute | solution.py:31
  6.1 1.3 collective-permute-start.17
  8.5 1.4 collective-permute-start
  9.9 5.2 %collective-permute-start.1 = (f32[1,64,1024]{2,1,0:T(8,128)S(1)}, f32[1,64,1024]{2,1,0:T(8,128)S(1)}, u32[]{:S(2)}, u32[]{:S(2)}) collective-permute-start(f32[1,64,1024]{2,1,0:T(8,128)S(1)} %get-tuple-element.53), channel_id=1, source_target_pairs={{0,2},{2,4},{4,6},{6,8},{8,10},{10,12},{12,14},{1,3},{3,5},{5,7},{... | collective-permute-start | bytes 786440 | tf_op jit(solution)/shard_map/ppermute | solution.py:31
  15.1 1.3 slice_bitcast_fusion
  16.4 2.5 collective-permute-done
  18.9 5.8 %collective-permute-done.1 = f32[1,64,1024]{2,1,0:T(8,128)S(1)} collective-permute-done((f32[1,64,1024]{2,1,0:T(8,128)S(1)}, f32[1,64,1024]{2,1,0:T(8,128)S(1)}, u32[]{:S(2)}, u32[]{:S(2)}) %collective-permute-start.1) | collective-permute-done | bytes 262176 | tf_op jit(solution)/shard_map/ppermute | solution.py:31
  25.3 1.3 collective-permute-start.2
  26.6 3.0 collective-permute-start.3
  32.0 1.2 copy.26
  34.3 1.2 copy.24
  36.5 1.2 copy.22
  38.9 1.8 copy-done
  40.7 4.5 %fusion.57 = f32[4,64,1024]{2,1,0:T(8,128)S(1)} fusion(f32[4,64,1024]{2,1,0:T(8,128)S(1)} %slice_bitcast_fusion, f32[6,66,1026]{2,1,0:T(8,128)S(1)} %select_maximum_fusion.12, f32[6,65,1024]{2,1,0:T(8,128)S(1)} %get-tuple-element.68, f32[6,65,1024]{2,1,0:T(8,128)S(1)} %get-tuple-element.67, f32[1,64,1024]{2,1,0:T(8,128)S(1)} %collective-permute-done.1, ...), kind=kLoop, calls=%fused_computation.129 | loop fusion | flops 18874368 | bytes 24117248 | tf_op jit(solution)/shard_map/add | solution.py:94
  45.3 1.3 collective-permute-start.4
  46.6 5.0 %collective-permute-start.5 = (f32[1,64,1024]{2,1,0:T(8,128)S(1)}, f32[1,64,1024]{2,1,0:T(8,128)S(1)}, u32[]{:S(2)}, u32[]{:S(2)}) collective-permute-start(f32[1,64,1024]{2,1,0:T(8,128)S(1)} %get-tuple-element.78), channel_id=1, source_target_pairs={{0,2},{2,4},{4,6},{6,8},{8,10},{10,12},{12,14},{1,3},{3,5},{5,7},{... | collective-permute-start | bytes 786440 | tf_op jit(solution)/shard_map/ppermute | solution.py:31
  52.5 3.1 collective-permute-done.4
  55.5 5.8 %collective-permute-done.5 = f32[1,64,1024]{2,1,0:T(8,128)S(1)} collective-permute-done((f32[1,64,1024]{2,1,0:T(8,128)S(1)}, f32[1,64,1024]{2,1,0:T(8,128)S(1)}, u32[]{:S(2)}, u32[]{:S(2)}) %collective-permute-start.5) | collective-permute-done | bytes 262176 | tf_op jit(solution)/shard_map/ppermute | solution.py:31
  61.3 1.3 collective-permute-start.6
  62.6 3.0 collective-permute-start.7
  65.7 1.3 collective-permute-start.19
  67.0 3.0 collective-permute-start.18
  71.2 6.3 %fusion.40 = f32[4,64,1024]{2,1,0:T(8,128)S(1)} fusion(f32[4,64,1024]{2,1,0:T(8,128)S(1)} %fusion.57, f32[6,66,1026]{2,1,0:T(8,128)S(1)} %select_maximum_fusion.8, f32[6,65,1024]{2,1,0:T(8,128)S(1)} %get-tuple-element.64, f32[6,65,1024]{2,1,0:T(8,128)S(1)} %get-tuple-element.63, f32[1,64,1024]{2,1,0:T(8,128)S(1)} %collective-permute-done.5, ...), kind=kLoop, calls=%fused_computation.98 | loop fusion | flops 33292288 | bytes 25165824 | tf_op jit(solution)/shard_map/add | solution.py:94
  77.5 1.3 collective-permute-start.8
  78.8 5.0 %collective-permute-start.9 = (f32[1,64,1024]{2,1,0:T(8,128)S(1)}, f32[1,64,1024]{2,1,0:T(8,128)S(1)}, u32[]{:S(2)}, u32[]{:S(2)}) collective-permute-start(f32[1,64,1024]{2,1,0:T(8,128)S(1)} %get-tuple-element.76), channel_id=1, source_target_pairs={{0,2},{2,4},{4,6},{6,8},{8,10},{10,12},{12,14},{1,3},{3,5},{5,7},{... | collective-permute-start | bytes 786440 | tf_op jit(solution)/shard_map/ppermute | solution.py:31
  84.1 3.6 %collective-permute-done.8 = f32[1,64,1024]{2,1,0:T(8,128)S(1)} collective-permute-done((f32[1,64,1024]{2,1,0:T(8,128)S(1)}, f32[1,64,1024]{2,1,0:T(8,128)S(1)}, u32[]{:S(2)}, u32[]{:S(2)}) %collective-permute-start.8) | collective-permute-done | bytes 262176 | tf_op jit(solution)/shard_map/ppermute | solution.py:32
  87.7 5.8 %collective-permute-done.9 = f32[1,64,1024]{2,1,0:T(8,128)S(1)} collective-permute-done((f32[1,64,1024]{2,1,0:T(8,128)S(1)}, f32[1,64,1024]{2,1,0:T(8,128)S(1)}, u32[]{:S(2)}, u32[]{:S(2)}) %collective-permute-start.9) | collective-permute-done | bytes 262176 | tf_op jit(solution)/shard_map/ppermute | solution.py:31
  93.5 1.3 collective-permute-start.10
  94.8 3.2 %collective-permute-start.11 = (f32[6,1,1024]{2,1,0:T(1,128)S(1)}, f32[6,1,1024]{2,1,0:T(1,128)S(1)}, u32[]{:S(2)}, u32[]{:S(2)}) collective-permute-start(f32[6,1,1024]{2,1,0:T(1,128)S(1)} %get-tuple-element.61), channel_id=1, source_target_pairs={{0,1},{2,3},{4,5},{6,7},{8,9},{10,11},{12,13},{14,15},{16,17},{18,... | collective-permute-start | bytes 73736 | tf_op jit(solution)/shard_map/ppermute | solution.py:31
  99.8 8.4 %fusion.23 = f32[4,64,1024]{2,1,0:T(8,128)S(1)} fusion(f32[4,64,1024]{2,1,0:T(8,128)S(1)} %fusion.40, f32[6,66,1026]{2,1,0:T(8,128)S(1)} %select_maximum_fusion.4, f32[6,65,1024]{2,1,0:T(8,128)S(1)} %get-tuple-element.60, f32[6,65,1024]{2,1,0:T(8,128)S(1)} %get-tuple-element.59, f32[1,64,1024]{2,1,0:T(8,128)S(1)} %collective-permute-done.9, ...), kind=kLoop, calls=%fused_computation.67 | loop fusion | flops 47710208 | bytes 26214400 | tf_op jit(solution)/shard_map/add | solution.py:94
  108.3 1.3 collective-permute-start.12
  109.6 5.0 %collective-permute-start.13 = (f32[1,64,1024]{2,1,0:T(8,128)S(1)}, f32[1,64,1024]{2,1,0:T(8,128)S(1)}, u32[]{:S(2)}, u32[]{:S(2)}) collective-permute-start(f32[1,64,1024]{2,1,0:T(8,128)S(1)} %get-tuple-element.74), channel_id=1, source_target_pairs={{0,2},{2,4},{4,6},{6,8},{8,10},{10,12},{12,14},{1,3},{3,5},{5,7},{... | collective-permute-start | bytes 786440 | tf_op jit(solution)/shard_map/ppermute | solution.py:31
  114.9 4.7 %collective-permute-done.12 = f32[1,64,1024]{2,1,0:T(8,128)S(1)} collective-permute-done((f32[1,64,1024]{2,1,0:T(8,128)S(1)}, f32[1,64,1024]{2,1,0:T(8,128)S(1)}, u32[]{:S(2)}, u32[]{:S(2)}) %collective-permute-start.12) | collective-permute-done | bytes 262176 | tf_op jit(solution)/shard_map/ppermute | solution.py:32
  119.5 5.8 %collective-permute-done.13 = f32[1,64,1024]{2,1,0:T(8,128)S(1)} collective-permute-done((f32[1,64,1024]{2,1,0:T(8,128)S(1)}, f32[1,64,1024]{2,1,0:T(8,128)S(1)}, u32[]{:S(2)}, u32[]{:S(2)}) %collective-permute-start.13) | collective-permute-done | bytes 262176 | tf_op jit(solution)/shard_map/ppermute | solution.py:31
  125.4 1.3 collective-permute-start.14
  126.7 3.0 collective-permute-start.15
  132.2 11.5 %fusion.6 = (f32[4,64,1024]{2,1,0:T(8,128)S(1)}, f32[4,64,1024]{2,1,0:T(8,128)}, f32[4,64,1024]{2,1,0:T(8,128)}, f32[4,64,1024]{2,1,0:T(8,128)}) fusion(f32[4,64,1024]{2,1,0:T(8,128)S(1)} %fusion.23, f32[6,66,1026]{2,1,0:T(8,128)S(1)} %select_maximum_fusion, f32[6,65,1024]{2,1,0:T(8,128)S(1)} %get-tuple-element.56, f32[6,65,1024]{2,1,0:T(8,128)S(1)} %get-tuple-element.55, ...), kind=kLoop, calls=%fused_computation.36 | loop fusion | flops 62128128 | bytes 30408704 | tf_op jit(solution)/shard_map/add | solution.py:94
  143.7 68.4 %reshape.2435 = f32[2,2,32,2,512,2]{5,4,3,2,1,0:T(8,128)} reshape(f32[4,64,1024]{2,1,0:T(8,128)S(1)} %get-tuple-element.49) | data formatting | bytes 2097152 | tf_op jit(solution)/shard_map/reshape | solution.py:108
  212.1 20.8 %reduce_sum.21 = f32[2,32,512]{2,1,0:T(8,128)S(1)} reduce(f32[2,2,32,2,512,2]{5,4,3,2,1,0:T(8,128)} %reshape.2435, f32[]{:T(128)} %constant.134.clone.1), dimensions={1,3,5}, to_apply=%region_0.1 | reduce | flops 229376 | bytes 1179652 | tf_op jit(solution)/shard_map/reduce_sum | solution.py:109
  233.6 5.5 %reduce_sum.27 = f32[16,2,256,2]{3,2,1,0:T(8,128)} reshape(f32[32,512]{1,0:T(8,128)S(1)} %get-tuple-element.47) | data formatting | bytes 131072 | tf_op jit(solution)/shard_map/reduce_sum | solution.py:109
  239.1 2.8 reduce_sum.28
  242.7 1.4 collective-permute-start.21
  244.2 5.0 %collective-permute-start.20 = (f32[9,1,16,256]{3,2,1,0:T(8,128)S(1)}, f32[9,1,16,256]{3,2,1,0:T(8,128)S(1)}, u32[]{:S(2)}, u32[]{:S(2)}) collective-permute-start(f32[9,1,16,256]{3,2,1,0:T(8,128)S(1)} %constant_dynamic-update-slice_fusion.3), channel_id=1, source_target_pairs={{0,2},{2,4},{4,6},{6,8},{8,10},{10,12},{12,14},{1,3},{3,5},{5,7},{... | collective-permute-start | bytes 442376 | tf_op jit(solution)/shard_map/ppermute | solution.py:31
  249.2 2.4 collective-permute-done.21
  251.6 3.3 %collective-permute-done.20 = f32[9,1,16,256]{3,2,1,0:T(8,128)S(1)} collective-permute-done((f32[9,1,16,256]{3,2,1,0:T(8,128)S(1)}, f32[9,1,16,256]{3,2,1,0:T(8,128)S(1)}, u32[]{:S(2)}, u32[]{:S(2)}) %collective-permute-start.20) | collective-permute-done | bytes 147488 | tf_op jit(solution)/shard_map/ppermute | solution.py:31
  255.0 1.3 collective-permute-start.23
  256.3 3.0 collective-permute-start.22
  261.0 1.3 collective-permute-start.25
  262.3 5.0 %collective-permute-start.24 = (f32[3,1,16,256]{3,2,1,0:T(8,128)S(1)}, f32[3,1,16,256]{3,2,1,0:T(8,128)S(1)}, u32[]{:S(2)}, u32[]{:S(2)}) collective-permute-start(f32[3,1,16,256]{3,2,1,0:T(8,128)S(1)} %fusion.155), channel_id=1, source_target_pairs={{0,2},{2,4},{4,6},{6,8},{8,10},{10,12},{12,14},{1,3},{3,5},{5,7},{... | collective-permute-start | bytes 147464 | tf_op jit(solution)/shard_map/ppermute | solution.py:31
  267.6 1.4 collective-permute-done.24
  269.1 1.3 collective-permute-start.27
  270.4 3.2 %collective-permute-start.26 = (f32[3,3,1,256]{3,2,1,0:T(1,128)S(1)}, f32[3,3,1,256]{3,2,1,0:T(1,128)S(1)}, u32[]{:S(2)}, u32[]{:S(2)}) collective-permute-start(f32[3,3,1,256]{3,2,1,0:T(1,128)S(1)} %get-tuple-element.98), channel_id=1, source_target_pairs={{0,1},{2,3},{4,5},{6,7},{8,9},{10,11},{12,13},{14,15},{16,17},{18,... | collective-permute-start | bytes 27656 | tf_op jit(solution)/shard_map/ppermute | solution.py:31
  275.6 1.3 collective-permute-start.29
  276.9 5.5 %collective-permute-start.28 = (f32[9,1,16,256]{3,2,1,0:T(8,128)S(1)}, f32[9,1,16,256]{3,2,1,0:T(8,128)S(1)}, u32[]{:S(2)}, u32[]{:S(2)}) collective-permute-start(f32[9,1,16,256]{3,2,1,0:T(8,128)S(1)} %constant_dynamic-update-slice_fusion.12), channel_id=1, source_target_pairs={{0,2},{2,4},{4,6},{6,8},{8,10},{10,12},{12,14},{1,3},{3,5},{5,7},{... | collective-permute-start | bytes 442376 | tf_op jit(solution)/shard_map/ppermute | solution.py:31
  282.3 2.4 collective-permute-done.29
  284.8 3.9 %collective-permute-done.28 = f32[9,1,16,256]{3,2,1,0:T(8,128)S(1)} collective-permute-done((f32[9,1,16,256]{3,2,1,0:T(8,128)S(1)}, f32[9,1,16,256]{3,2,1,0:T(8,128)S(1)}, u32[]{:S(2)}, u32[]{:S(2)}) %collective-permute-start.28) | collective-permute-done | bytes 147488 | tf_op jit(solution)/shard_map/ppermute | solution.py:31
  288.7 1.3 collective-permute-start.31
  290.1 3.3 %collective-permute-start.30 = (f32[9,3,1,256]{3,2,1,0:T(1,128)S(1)}, f32[9,3,1,256]{3,2,1,0:T(1,128)S(1)}, u32[]{:S(2)}, u32[]{:S(2)}) collective-permute-start(f32[9,3,1,256]{3,2,1,0:T(1,128)S(1)} %get-tuple-element.86), channel_id=1, source_target_pairs={{0,1},{2,3},{4,5},{6,7},{8,9},{10,11},{12,13},{14,15},{16,17},{18,... | collective-permute-start | bytes 82952 | tf_op jit(solution)/shard_map/ppermute | solution.py:31
  295.1 1.3 collective-permute-start.33
  296.4 5.0 %collective-permute-start.32 = (f32[3,1,16,256]{3,2,1,0:T(8,128)S(1)}, f32[3,1,16,256]{3,2,1,0:T(8,128)S(1)}, u32[]{:S(2)}, u32[]{:S(2)}) collective-permute-start(f32[3,1,16,256]{3,2,1,0:T(8,128)S(1)} %fusion.139), channel_id=1, source_target_pairs={{0,2},{2,4},{4,6},{6,8},{8,10},{10,12},{12,14},{1,3},{3,5},{5,7},{... | collective-permute-start | bytes 147464 | tf_op jit(solution)/shard_map/ppermute | solution.py:31
  301.4 2.2 add_bitcast_fusion.2
  303.7 1.3 collective-permute-start.35
  305.0 3.0 collective-permute-start.34
  308.0 2.4 pad_maximum_fusion
  (159 shorter events, 23.6 us)
Async XLA Ops:
  0.6 51.0 %collective-permute-start.16 = (f32[3,1,16,256]{3,2,1,0:T(8,128)}, f32[3,1,16,256]{3,2,1,0:T(8,128)}, u32[]{:S(2)}, u32[]{:S(2)}) collective-permute-start(f32[3,1,16,256]{3,2,1,0:T(8,128)} %param.9), channel_id=1, source_target_pairs={{0,2},{2,4},{4,6},{6,8},{8,10},{10,12},{12,14},{1,3},{3,5},{5,7},{... | collective-permute-start | bytes 147464 | tf_op jit(solution)/shard_map/ppermute | solution.py:31
  6.1 46.4 %collective-permute-start.17 = (f32[3,1,16,256]{3,2,1,0:T(8,128)}, f32[3,1,16,256]{3,2,1,0:T(8,128)S(1)}, u32[]{:S(2)}, u32[]{:S(2)}) collective-permute-start(f32[3,1,16,256]{3,2,1,0:T(8,128)} %param.9), channel_id=1, source_target_pairs={{2,0},{4,2},{6,4},{8,6},{10,8},{12,10},{14,12},{3,1},{5,3},{7,5},{... | collective-permute-start | bytes 147464 | tf_op jit(solution)/shard_map/ppermute | solution.py:32
  8.5 21.2 %copy-start.12 = (f32[6,1,16,256]{3,2,1,0:T(8,128)S(1)}, f32[6,1,16,256]{3,2,1,0:T(8,128)}, u32[]{:S(2)}) copy-start(f32[6,1,16,256]{3,2,1,0:T(8,128)} %param.6) | copy-start | bytes 294916
  8.5 10.4 %collective-permute-start = (f32[1,64,1024]{2,1,0:T(8,128)S(1)}, f32[1,64,1024]{2,1,0:T(8,128)S(1)}, u32[]{:S(2)}, u32[]{:S(2)}) collective-permute-start(f32[1,64,1024]{2,1,0:T(8,128)S(1)} %get-tuple-element.54), channel_id=1, source_target_pairs={{2,0},{4,2},{6,4},{8,6},{10,8},{12,10},{14,12},{3,1},{5,3},{7,5},{... | collective-permute-start | bytes 786440 | tf_op jit(solution)/shard_map/ppermute | solution.py:32
  9.9 14.8 %collective-permute-start.1 = (f32[1,64,1024]{2,1,0:T(8,128)S(1)}, f32[1,64,1024]{2,1,0:T(8,128)S(1)}, u32[]{:S(2)}, u32[]{:S(2)}) collective-permute-start(f32[1,64,1024]{2,1,0:T(8,128)S(1)} %get-tuple-element.53), channel_id=1, source_target_pairs={{0,2},{2,4},{4,6},{6,8},{8,10},{10,12},{12,14},{1,3},{3,5},{5,7},{... | collective-permute-start | bytes 786440 | tf_op jit(solution)/shard_map/ppermute | solution.py:31
  25.3 12.5 %collective-permute-start.2 = (f32[6,1,1024]{2,1,0:T(1,128)}, f32[6,1,1024]{2,1,0:T(1,128)S(1)}, u32[]{:S(2)}, u32[]{:S(2)}) collective-permute-start(f32[6,1,1024]{2,1,0:T(1,128)} %get-tuple-element.70), channel_id=1, source_target_pairs={{1,0},{3,2},{5,4},{7,6},{9,8},{11,10},{13,12},{15,14},{17,16},{19,... | collective-permute-start | bytes 73736 | tf_op jit(solution)/shard_map/ppermute | solution.py:32
  26.6 11.2 %collective-permute-start.3 = (f32[6,1,1024]{2,1,0:T(1,128)}, f32[6,1,1024]{2,1,0:T(1,128)S(1)}, u32[]{:S(2)}, u32[]{:S(2)}) collective-permute-start(f32[6,1,1024]{2,1,0:T(1,128)} %get-tuple-element.69), channel_id=1, source_target_pairs={{0,1},{2,3},{4,5},{6,7},{8,9},{10,11},{12,13},{14,15},{16,17},{18,... | collective-permute-start | bytes 73736 | tf_op jit(solution)/shard_map/ppermute | solution.py:31
  37.8 62.1 %copy-start.1 = (f32[64,1024]{1,0:T(8,128)}, f32[64,1024]{1,0:T(8,128)S(1)}, u32[]{:S(2)}) copy-start(f32[64,1024]{1,0:T(8,128)S(1)} %copy.22) | copy-start | bytes 786436
  38.5 2.2 copy-start
  40.7 11.7 %copy-start.9 = (f32[3,1,16,256]{3,2,1,0:T(8,128)S(1)}, f32[3,1,16,256]{3,2,1,0:T(8,128)}, u32[]{:S(2)}) copy-start(f32[3,1,16,256]{3,2,1,0:T(8,128)} %param.9) | copy-start | bytes 147460
  45.3 10.2 %collective-permute-start.4 = (f32[1,64,1024]{2,1,0:T(8,128)S(1)}, f32[1,64,1024]{2,1,0:T(8,128)S(1)}, u32[]{:S(2)}, u32[]{:S(2)}) collective-permute-start(f32[1,64,1024]{2,1,0:T(8,128)S(1)} %get-tuple-element.79), channel_id=1, source_target_pairs={{2,0},{4,2},{6,4},{8,6},{10,8},{12,10},{14,12},{3,1},{5,3},{7,5},{... | collective-permute-start | bytes 786440 | tf_op jit(solution)/shard_map/ppermute | solution.py:32
  46.6 14.7 %collective-permute-start.5 = (f32[1,64,1024]{2,1,0:T(8,128)S(1)}, f32[1,64,1024]{2,1,0:T(8,128)S(1)}, u32[]{:S(2)}, u32[]{:S(2)}) collective-permute-start(f32[1,64,1024]{2,1,0:T(8,128)S(1)} %get-tuple-element.78), channel_id=1, source_target_pairs={{0,2},{2,4},{4,6},{6,8},{8,10},{10,12},{12,14},{1,3},{3,5},{5,7},{... | collective-permute-start | bytes 786440 | tf_op jit(solution)/shard_map/ppermute | solution.py:31
  61.3 8.7 %collective-permute-start.6 = (f32[6,1,1024]{2,1,0:T(1,128)S(1)}, f32[6,1,1024]{2,1,0:T(1,128)S(1)}, u32[]{:S(2)}, u32[]{:S(2)}) collective-permute-start(f32[6,1,1024]{2,1,0:T(1,128)S(1)} %get-tuple-element.66), channel_id=1, source_target_pairs={{1,0},{3,2},{5,4},{7,6},{9,8},{11,10},{13,12},{15,14},{17,16},{19,... | collective-permute-start | bytes 73736 | tf_op jit(solution)/shard_map/ppermute | solution.py:32
  62.6 7.4 %collective-permute-start.7 = (f32[6,1,1024]{2,1,0:T(1,128)S(1)}, f32[6,1,1024]{2,1,0:T(1,128)S(1)}, u32[]{:S(2)}, u32[]{:S(2)}) collective-permute-start(f32[6,1,1024]{2,1,0:T(1,128)S(1)} %get-tuple-element.65), channel_id=1, source_target_pairs={{0,1},{2,3},{4,5},{6,7},{8,9},{10,11},{12,13},{14,15},{16,17},{18,... | collective-permute-start | bytes 73736 | tf_op jit(solution)/shard_map/ppermute | solution.py:31
  65.7 18.2 %collective-permute-start.19 = (f32[3,3,1,256]{3,2,1,0:T(1,128)S(1)}, f32[3,3,1,256]{3,2,1,0:T(1,128)S(1)}, u32[]{:S(2)}, u32[]{:S(2)}) collective-permute-start(f32[3,3,1,256]{3,2,1,0:T(1,128)S(1)} %get-tuple-element.101), channel_id=1, source_target_pairs={{1,0},{3,2},{5,4},{7,6},{9,8},{11,10},{13,12},{15,14},{17,16},{19,... | collective-permute-start | bytes 27656 | tf_op jit(solution)/shard_map/ppermute | solution.py:32
  67.0 16.9 %collective-permute-start.18 = (f32[3,3,1,256]{3,2,1,0:T(1,128)S(1)}, f32[3,3,1,256]{3,2,1,0:T(1,128)S(1)}, u32[]{:S(2)}, u32[]{:S(2)}) collective-permute-start(f32[3,3,1,256]{3,2,1,0:T(1,128)S(1)} %get-tuple-element.100), channel_id=1, source_target_pairs={{0,1},{2,3},{4,5},{6,7},{8,9},{10,11},{12,13},{14,15},{16,17},{18,... | collective-permute-start | bytes 27656 | tf_op jit(solution)/shard_map/ppermute | solution.py:31
  77.5 10.2 %collective-permute-start.8 = (f32[1,64,1024]{2,1,0:T(8,128)S(1)}, f32[1,64,1024]{2,1,0:T(8,128)S(1)}, u32[]{:S(2)}, u32[]{:S(2)}) collective-permute-start(f32[1,64,1024]{2,1,0:T(8,128)S(1)} %get-tuple-element.77), channel_id=1, source_target_pairs={{2,0},{4,2},{6,4},{8,6},{10,8},{12,10},{14,12},{3,1},{5,3},{7,5},{... | collective-permute-start | bytes 786440 | tf_op jit(solution)/shard_map/ppermute | solution.py:32
  78.8 14.7 %collective-permute-start.9 = (f32[1,64,1024]{2,1,0:T(8,128)S(1)}, f32[1,64,1024]{2,1,0:T(8,128)S(1)}, u32[]{:S(2)}, u32[]{:S(2)}) collective-permute-start(f32[1,64,1024]{2,1,0:T(8,128)S(1)} %get-tuple-element.76), channel_id=1, source_target_pairs={{0,2},{2,4},{4,6},{6,8},{8,10},{10,12},{12,14},{1,3},{3,5},{5,7},{... | collective-permute-start | bytes 786440 | tf_op jit(solution)/shard_map/ppermute | solution.py:31
  93.5 4.6 %collective-permute-start.10 = (f32[6,1,1024]{2,1,0:T(1,128)S(1)}, f32[6,1,1024]{2,1,0:T(1,128)S(1)}, u32[]{:S(2)}, u32[]{:S(2)}) collective-permute-start(f32[6,1,1024]{2,1,0:T(1,128)S(1)} %get-tuple-element.62), channel_id=1, source_target_pairs={{1,0},{3,2},{5,4},{7,6},{9,8},{11,10},{13,12},{15,14},{17,16},{19,... | collective-permute-start | bytes 73736 | tf_op jit(solution)/shard_map/ppermute | solution.py:32
  94.8 3.9 %collective-permute-start.11 = (f32[6,1,1024]{2,1,0:T(1,128)S(1)}, f32[6,1,1024]{2,1,0:T(1,128)S(1)}, u32[]{:S(2)}, u32[]{:S(2)}) collective-permute-start(f32[6,1,1024]{2,1,0:T(1,128)S(1)} %get-tuple-element.61), channel_id=1, source_target_pairs={{0,1},{2,3},{4,5},{6,7},{8,9},{10,11},{12,13},{14,15},{16,17},{18,... | collective-permute-start | bytes 73736 | tf_op jit(solution)/shard_map/ppermute | solution.py:31
  108.3 11.2 %collective-permute-start.12 = (f32[1,64,1024]{2,1,0:T(8,128)S(1)}, f32[1,64,1024]{2,1,0:T(8,128)S(1)}, u32[]{:S(2)}, u32[]{:S(2)}) collective-permute-start(f32[1,64,1024]{2,1,0:T(8,128)S(1)} %get-tuple-element.75), channel_id=1, source_target_pairs={{2,0},{4,2},{6,4},{8,6},{10,8},{12,10},{14,12},{3,1},{5,3},{7,5},{... | collective-permute-start | bytes 786440 | tf_op jit(solution)/shard_map/ppermute | solution.py:32
  109.6 15.7 %collective-permute-start.13 = (f32[1,64,1024]{2,1,0:T(8,128)S(1)}, f32[1,64,1024]{2,1,0:T(8,128)S(1)}, u32[]{:S(2)}, u32[]{:S(2)}) collective-permute-start(f32[1,64,1024]{2,1,0:T(8,128)S(1)} %get-tuple-element.74), channel_id=1, source_target_pairs={{0,2},{2,4},{4,6},{6,8},{8,10},{10,12},{12,14},{1,3},{3,5},{5,7},{... | collective-permute-start | bytes 786440 | tf_op jit(solution)/shard_map/ppermute | solution.py:31
  125.4 5.1 %collective-permute-start.14 = (f32[6,1,1024]{2,1,0:T(1,128)S(1)}, f32[6,1,1024]{2,1,0:T(1,128)S(1)}, u32[]{:S(2)}, u32[]{:S(2)}) collective-permute-start(f32[6,1,1024]{2,1,0:T(1,128)S(1)} %get-tuple-element.58), channel_id=1, source_target_pairs={{1,0},{3,2},{5,4},{7,6},{9,8},{11,10},{13,12},{15,14},{17,16},{19,... | collective-permute-start | bytes 73736 | tf_op jit(solution)/shard_map/ppermute | solution.py:32
  126.7 3.9 %collective-permute-start.15 = (f32[6,1,1024]{2,1,0:T(1,128)S(1)}, f32[6,1,1024]{2,1,0:T(1,128)S(1)}, u32[]{:S(2)}, u32[]{:S(2)}) collective-permute-start(f32[6,1,1024]{2,1,0:T(1,128)S(1)} %get-tuple-element.57), channel_id=1, source_target_pairs={{0,1},{2,3},{4,5},{6,7},{8,9},{10,11},{12,13},{14,15},{16,17},{18,... | collective-permute-start | bytes 73736 | tf_op jit(solution)/shard_map/ppermute | solution.py:31
  131.3 1.0 copy-start.2
  212.1 20.8 %copy-start.11 = (f32[2,32,512]{2,1,0:T(8,128)S(1)}, f32[2,32,512]{2,1,0:T(8,128)}, u32[]{:S(2)}) copy-start(f32[2,32,512]{2,1,0:T(8,128)} %param.7) | copy-start | bytes 393220
  239.1 2.8 copy-start.6
  239.1 2.8 copy-start.7
  242.7 18.1 %copy-start.10 = (f32[3,1,16,256]{3,2,1,0:T(8,128)S(1)}, f32[3,1,16,256]{3,2,1,0:T(8,128)}, u32[]{:S(2)}) copy-start(f32[3,1,16,256]{3,2,1,0:T(8,128)} %param.9) | copy-start | bytes 147460
  242.7 8.9 %collective-permute-start.21 = (f32[9,1,16,256]{3,2,1,0:T(8,128)S(1)}, f32[9,1,16,256]{3,2,1,0:T(8,128)S(1)}, u32[]{:S(2)}, u32[]{:S(2)}) collective-permute-start(f32[9,1,16,256]{3,2,1,0:T(8,128)S(1)} %constant_dynamic-update-slice_fusion.3), channel_id=1, source_target_pairs={{2,0},{4,2},{6,4},{8,6},{10,8},{12,10},{14,12},{3,1},{5,3},{7,5},{... | collective-permute-start | bytes 442376 | tf_op jit(solution)/shard_map/ppermute | solution.py:32
  244.2 10.8 %collective-permute-start.20 = (f32[9,1,16,256]{3,2,1,0:T(8,128)S(1)}, f32[9,1,16,256]{3,2,1,0:T(8,128)S(1)}, u32[]{:S(2)}, u32[]{:S(2)}) collective-permute-start(f32[9,1,16,256]{3,2,1,0:T(8,128)S(1)} %constant_dynamic-update-slice_fusion.3), channel_id=1, source_target_pairs={{0,2},{2,4},{4,6},{6,8},{8,10},{10,12},{12,14},{1,3},{3,5},{5,7},{... | collective-permute-start | bytes 442376 | tf_op jit(solution)/shard_map/ppermute | solution.py:31
  255.0 4.3 %collective-permute-start.23 = (f32[9,3,1,256]{3,2,1,0:T(1,128)S(1)}, f32[9,3,1,256]{3,2,1,0:T(1,128)S(1)}, u32[]{:S(2)}, u32[]{:S(2)}) collective-permute-start(f32[9,3,1,256]{3,2,1,0:T(1,128)S(1)} %get-tuple-element.89), channel_id=1, source_target_pairs={{1,0},{3,2},{5,4},{7,6},{9,8},{11,10},{13,12},{15,14},{17,16},{19,... | collective-permute-start | bytes 82952 | tf_op jit(solution)/shard_map/ppermute | solution.py:32
  256.3 3.9 %collective-permute-start.22 = (f32[9,3,1,256]{3,2,1,0:T(1,128)S(1)}, f32[9,3,1,256]{3,2,1,0:T(1,128)S(1)}, u32[]{:S(2)}, u32[]{:S(2)}) collective-permute-start(f32[9,3,1,256]{3,2,1,0:T(1,128)S(1)} %get-tuple-element.88), channel_id=1, source_target_pairs={{0,1},{2,3},{4,5},{6,7},{8,9},{10,11},{12,13},{14,15},{16,17},{18,... | collective-permute-start | bytes 82952 | tf_op jit(solution)/shard_map/ppermute | solution.py:31
  261.0 6.6 %collective-permute-start.25 = (f32[3,1,16,256]{3,2,1,0:T(8,128)S(1)}, f32[3,1,16,256]{3,2,1,0:T(8,128)S(1)}, u32[]{:S(2)}, u32[]{:S(2)}) collective-permute-start(f32[3,1,16,256]{3,2,1,0:T(8,128)S(1)} %fusion.155), channel_id=1, source_target_pairs={{2,0},{4,2},{6,4},{8,6},{10,8},{12,10},{14,12},{3,1},{5,3},{7,5},{... | collective-permute-start | bytes 147464 | tf_op jit(solution)/shard_map/ppermute | solution.py:32
  262.3 6.7 %collective-permute-start.24 = (f32[3,1,16,256]{3,2,1,0:T(8,128)S(1)}, f32[3,1,16,256]{3,2,1,0:T(8,128)S(1)}, u32[]{:S(2)}, u32[]{:S(2)}) collective-permute-start(f32[3,1,16,256]{3,2,1,0:T(8,128)S(1)} %fusion.155), channel_id=1, source_target_pairs={{0,2},{2,4},{4,6},{6,8},{8,10},{10,12},{12,14},{1,3},{3,5},{5,7},{... | collective-permute-start | bytes 147464 | tf_op jit(solution)/shard_map/ppermute | solution.py:31
  269.1 4.6 %collective-permute-start.27 = (f32[3,3,1,256]{3,2,1,0:T(1,128)S(1)}, f32[3,3,1,256]{3,2,1,0:T(1,128)S(1)}, u32[]{:S(2)}, u32[]{:S(2)}) collective-permute-start(f32[3,3,1,256]{3,2,1,0:T(1,128)S(1)} %get-tuple-element.99), channel_id=1, source_target_pairs={{1,0},{3,2},{5,4},{7,6},{9,8},{11,10},{13,12},{15,14},{17,16},{19,... | collective-permute-start | bytes 27656 | tf_op jit(solution)/shard_map/ppermute | solution.py:32
  270.4 3.8 %collective-permute-start.26 = (f32[3,3,1,256]{3,2,1,0:T(1,128)S(1)}, f32[3,3,1,256]{3,2,1,0:T(1,128)S(1)}, u32[]{:S(2)}, u32[]{:S(2)}) collective-permute-start(f32[3,3,1,256]{3,2,1,0:T(1,128)S(1)} %get-tuple-element.98), channel_id=1, source_target_pairs={{0,1},{2,3},{4,5},{6,7},{8,9},{10,11},{12,13},{14,15},{16,17},{18,... | collective-permute-start | bytes 27656 | tf_op jit(solution)/shard_map/ppermute | solution.py:31
  275.6 9.2 %collective-permute-start.29 = (f32[9,1,16,256]{3,2,1,0:T(8,128)S(1)}, f32[9,1,16,256]{3,2,1,0:T(8,128)S(1)}, u32[]{:S(2)}, u32[]{:S(2)}) collective-permute-start(f32[9,1,16,256]{3,2,1,0:T(8,128)S(1)} %constant_dynamic-update-slice_fusion.12), channel_id=1, source_target_pairs={{2,0},{4,2},{6,4},{8,6},{10,8},{12,10},{14,12},{3,1},{5,3},{7,5},{... | collective-permute-start | bytes 442376 | tf_op jit(solution)/shard_map/ppermute | solution.py:32
  276.9 11.8 %collective-permute-start.28 = (f32[9,1,16,256]{3,2,1,0:T(8,128)S(1)}, f32[9,1,16,256]{3,2,1,0:T(8,128)S(1)}, u32[]{:S(2)}, u32[]{:S(2)}) collective-permute-start(f32[9,1,16,256]{3,2,1,0:T(8,128)S(1)} %constant_dynamic-update-slice_fusion.12), channel_id=1, source_target_pairs={{0,2},{2,4},{4,6},{6,8},{8,10},{10,12},{12,14},{1,3},{3,5},{5,7},{... | collective-permute-start | bytes 442376 | tf_op jit(solution)/shard_map/ppermute | solution.py:31
  288.7 4.6 %collective-permute-start.31 = (f32[9,3,1,256]{3,2,1,0:T(1,128)S(1)}, f32[9,3,1,256]{3,2,1,0:T(1,128)S(1)}, u32[]{:S(2)}, u32[]{:S(2)}) collective-permute-start(f32[9,3,1,256]{3,2,1,0:T(1,128)S(1)} %get-tuple-element.87), channel_id=1, source_target_pairs={{1,0},{3,2},{5,4},{7,6},{9,8},{11,10},{13,12},{15,14},{17,16},{19,... | collective-permute-start | bytes 82952 | tf_op jit(solution)/shard_map/ppermute | solution.py:32
  290.0 11.4 %copy-start.3 = (f32[4,64,1024]{2,1,0:T(8,128)S(1)}, f32[4,64,1024]{2,1,0:T(8,128)}, u32[]{:S(2)}) copy-start(f32[4,64,1024]{2,1,0:T(8,128)} %get-tuple-element.50) | copy-start | bytes 3145732
  290.0 11.4 %copy-start.4 = (f32[4,64,1024]{2,1,0:T(8,128)S(1)}, f32[4,64,1024]{2,1,0:T(8,128)}, u32[]{:S(2)}) copy-start(f32[4,64,1024]{2,1,0:T(8,128)} %get-tuple-element.51) | copy-start | bytes 3145732
  290.1 11.4 %copy-start.5 = (f32[4,64,1024]{2,1,0:T(8,128)S(1)}, f32[4,64,1024]{2,1,0:T(8,128)}, u32[]{:S(2)}) copy-start(f32[4,64,1024]{2,1,0:T(8,128)} %get-tuple-element.52) | copy-start | bytes 3145732
  290.1 4.1 %collective-permute-start.30 = (f32[9,3,1,256]{3,2,1,0:T(1,128)S(1)}, f32[9,3,1,256]{3,2,1,0:T(1,128)S(1)}, u32[]{:S(2)}, u32[]{:S(2)}) collective-permute-start(f32[9,3,1,256]{3,2,1,0:T(1,128)S(1)} %get-tuple-element.86), channel_id=1, source_target_pairs={{0,1},{2,3},{4,5},{6,7},{8,9},{10,11},{12,13},{14,15},{16,17},{18,... | collective-permute-start | bytes 82952 | tf_op jit(solution)/shard_map/ppermute | solution.py:31
  295.1 15.3 %copy-start.8 = (f32[3,1,16,256]{3,2,1,0:T(8,128)}, f32[3,1,16,256]{3,2,1,0:T(8,128)S(1)}, u32[]{:S(2)}) copy-start(f32[3,1,16,256]{3,2,1,0:T(8,128)S(1)} %fusion.139) | copy-start | bytes 147460
  295.1 8.5 %collective-permute-start.33 = (f32[3,1,16,256]{3,2,1,0:T(8,128)S(1)}, f32[3,1,16,256]{3,2,1,0:T(8,128)S(1)}, u32[]{:S(2)}, u32[]{:S(2)}) collective-permute-start(f32[3,1,16,256]{3,2,1,0:T(8,128)S(1)} %fusion.139), channel_id=1, source_target_pairs={{2,0},{4,2},{6,4},{8,6},{10,8},{12,10},{14,12},{3,1},{5,3},{7,5},{... | collective-permute-start | bytes 147464 | tf_op jit(solution)/shard_map/ppermute | solution.py:32
  296.4 7.2 %collective-permute-start.32 = (f32[3,1,16,256]{3,2,1,0:T(8,128)S(1)}, f32[3,1,16,256]{3,2,1,0:T(8,128)S(1)}, u32[]{:S(2)}, u32[]{:S(2)}) collective-permute-start(f32[3,1,16,256]{3,2,1,0:T(8,128)S(1)} %fusion.139), channel_id=1, source_target_pairs={{0,2},{2,4},{4,6},{6,8},{8,10},{10,12},{12,14},{1,3},{3,5},{5,7},{... | collective-permute-start | bytes 147464 | tf_op jit(solution)/shard_map/ppermute | solution.py:31
  303.7 6.7 %collective-permute-start.35 = (f32[3,3,1,256]{3,2,1,0:T(1,128)S(1)}, f32[3,3,1,256]{3,2,1,0:T(1,128)S(1)}, u32[]{:S(2)}, u32[]{:S(2)}) collective-permute-start(f32[3,3,1,256]{3,2,1,0:T(1,128)S(1)} %get-tuple-element.97), channel_id=1, source_target_pairs={{1,0},{3,2},{5,4},{7,6},{9,8},{11,10},{13,12},{15,14},{17,16},{19,... | collective-permute-start | bytes 27656 | tf_op jit(solution)/shard_map/ppermute | solution.py:32
  305.0 5.4 %collective-permute-start.34 = (f32[3,3,1,256]{3,2,1,0:T(1,128)S(1)}, f32[3,3,1,256]{3,2,1,0:T(1,128)S(1)}, u32[]{:S(2)}, u32[]{:S(2)}) collective-permute-start(f32[3,3,1,256]{3,2,1,0:T(1,128)S(1)} %get-tuple-element.96), channel_id=1, source_target_pairs={{0,1},{2,3},{4,5},{6,7},{8,9},{10,11},{12,13},{14,15},{16,17},{18,... | collective-permute-start | bytes 27656 | tf_op jit(solution)/shard_map/ppermute | solution.py:31
  312.4 0.6 copy-start.13
where the time goes:
time: 315 us; the launch traced here: 313 us
  starting transfers between devices  97.6 us (31%)
  local copies, waits for them, and re-layouts  88.1 us (28%)
  other arithmetic  71.7 us (23%)
  waiting for transfers between devices  53.7 us (17%)
    ppermute x18, starting transfers between devices, extended(): before = lax.ppermute(last, axis, up)  74.1 us
    reshape x1, local copies, waits for them, and re-layouts, coarsen(): field.reshape(field.shape[0] // 2, 2, field.shape[1] // 2, 2, field.shape...  68.4 us
    ppermute x18, waiting for transfers between devices, extended(): before = lax.ppermute(last, axis, up)  34.7 us
    add x4, other arithmetic, excite_step(): new_volt = volt + diffusion(padded, coeff) + STEP_TIME * ion  30.7 us
    reduce_sum x3, other arithmetic, coarsen(): return jnp.mean(shaped, axis=(1, 3, 5))  24.3 us
    ppermute x18, starting transfers between devices, extended(): after = lax.ppermute(initial, axis, down)  23.5 us
    ppermute x18, waiting for transfers between devices, extended(): after = lax.ppermute(initial, axis, down)  19 us
    concatenate x17, other arithmetic, extended(): array = jnp.concatenate([before, array, after], axis=dim)  6.91 us
  transfers between devices with their start and end apart: 36, of which 19 were waited for; matrix products, arithmetic and copies ran while one was open for 10% of the time, Pallas kernels for 0%

commit v1 on v0

v1 whole, which is shorter than its diff:
```python
import functools

import jax
import jax.numpy as jnp
from jax import lax
from jax.experimental import pallas as pl
from jax.experimental.pallas import tpu as pltpu
from jax.sharding import PartitionSpec as P

SUB = 4
MECH_STEPS = 2
NFIB = 64
STEP_TIME = 0.05
MECH_RATE = 0.15
SIGMA_LONG = 0.16
SIGMA_TRANS = 0.04
PAIRS = ((0, 0), (1, 1), (2, 2), (0, 1), (0, 2), (1, 2))
MESH = pl.DeviceIdType.MESH
HI = lax.Precision.HIGHEST
F32 = jnp.float32
TILE = 8
CHUNK = 256


def ionic(u, v, w, s):
    th_v = jnp.tanh(50.0 * (u - 0.3))
    th_w = jnp.tanh(50.0 * (u - 0.13))
    th_o = jnp.tanh(50.0 * (u - 0.006))
    th_m = jnp.tanh(65.0 * (u - 0.03))
    th_s = jnp.tanh(2.0458 * (u - 0.65))
    th_r = jnp.tanh(2.0994 * (u - 0.9087))
    hv = 0.5 + 0.5 * th_v
    hw = 0.5 + 0.5 * th_w
    ho = 0.5 + 0.5 * th_o
    nv = 1.0 - hv
    nw = 1.0 - hw
    no = 1.0 - ho
    tau_v = 605.0 + 545.0 * th_o
    tau_w = 37.5 - 22.5 * th_m
    tau_so = 15.5069 - 14.5112 * th_s
    tau_s = 9.3671 + 6.6329 * th_w
    tau_o = 203.0 - 197.0 * th_o
    w_inf = no * (1.0 - u * (1.0 / 0.07)) + 0.94 * ho
    fast = v * hv * (u - 0.3) * (1.55 - u) * (STEP_TIME / 0.11)
    slow = hw * (w * s) * (STEP_TIME / 1.8875)
    out = (u * nw * tau_so + hw * tau_o) * (STEP_TIME / (tau_o * tau_so))
    du = fast - out + slow
    inv = STEP_TIME / (tau_v * tau_w)
    v2 = v + nv * (no - v) * (tau_w * inv) - hv * v * (STEP_TIME / 1.4506)
    w2 = w + nw * (w_inf - w) * (tau_v * inv) - hw * w * (STEP_TIME / 200.0)
    s2 = s + (0.5 + 0.5 * th_r - s) * (STEP_TIME / tau_s)
    return du, v2, w2, s2


def iota2(shape, dim):
    return lax.broadcasted_iota(jnp.int32, shape, dim)


def excite_kernel(
    slabs, states, cond, tension, out, ten_out, act_out,
    ubuf, coeff, dif, load_sem, sz, rz, sc, rc, sy, ry,
):
    grp = lax.axis_index("grp")
    slab = lax.axis_index("slab")
    col = lax.axis_index("col")
    other = 1 - col
    depth, rows, width = out.shape[1:]
    tiles = rows // TILE
    has_up = slab < slabs - 1
    has_dn = slab > 0
    edge_src = rows - (rows - TILE) * col
    edge_dst = (rows + TILE) * col

    load_u = pltpu.make_async_copy(
        states.at[0], ubuf.at[0, pl.ds(1, depth), pl.ds(TILE, rows), :], load_sem.at[0]
    )
    load_g = pltpu.make_async_copy(
        states.at[pl.ds(1, 3)], out.at[pl.ds(1, 3)], load_sem.at[1]
    )
    load_u.start()
    load_g.start()

    barrier = pltpu.get_barrier_semaphore()

    def greet(where):
        pl.semaphore_signal(barrier, inc=1, device_id=where, device_id_type=MESH)

    greet((grp, slab, other))

    @pl.when(has_up)
    def _():
        greet((grp, slab + 1, col))
        greet((grp, slab + 1, other))

    @pl.when(has_dn)
    def _():
        greet((grp, slab - 1, col))
        greet((grp, slab - 1, other))

    blank = jnp.zeros((TILE, width), F32)

    def clear_y(n, c):
        ubuf[n // (depth + 2), n % (depth + 2), pl.ds(pl.multiple_of(edge_dst, TILE), TILE), :] = blank
        return c

    lax.fori_loop(0, SUB * (depth + 2), clear_y, 0)

    def clear_z(layer):
        per = rows // TILE + 2

        def body(n, c):
            ubuf[n // per, layer, pl.ds(pl.multiple_of((n % per) * TILE, TILE), TILE), :] = blank
            return c

        lax.fori_loop(0, SUB * per, body, 0)

    @pl.when(slab == 0)
    def _():
        clear_z(0)

    @pl.when(slab == slabs - 1)
    def _():
        clear_z(depth + 1)

    spread_x = (iota2((128, 512), 0) == iota2((128, 512), 1) // 4).astype(F32)
    spread_y = (iota2((rows, rows // 4), 0) // 4 == iota2((rows, rows // 4), 1)).astype(F32)
    for c in range(6):
        for h in range(width // 512):
            part = jnp.dot(
                cond[c, 0, :, h * 128 : (h + 1) * 128], spread_x, precision=HI,
                preferred_element_type=F32,
            )
            part = jnp.dot(spread_y, part, precision=HI, preferred_element_type=F32)
            coeff[c, :, h * 512 : (h + 1) * 512] = part if c < 3 else 0.5 * part

    def row_of(step):
        return jnp.where(col == 1, step, tiles - 1 - step)

    def copy_z(slot, way, step):
        at = pl.ds(pl.multiple_of(TILE + TILE * row_of(step), TILE), TILE)
        src = depth if way == 0 else 1
        dst = 0 if way == 0 else depth + 1
        to = slab + 1 if way == 0 else slab - 1
        return pltpu.make_async_remote_copy(
            src_ref=ubuf.at[slot, src, at, :],
            dst_ref=ubuf.at[slot, dst, at, :],
            send_sem=sz.at[slot, way, step],
            recv_sem=rz.at[slot, way, step],
            device_id=(grp, to, col),
            device_id_type=MESH,
        )

    def copy_c(slot, way):
        src = depth if way == 0 else 1
        dst = 0 if way == 0 else depth + 1
        to = slab + 1 if way == 0 else slab - 1
        return pltpu.make_async_remote_copy(
            src_ref=ubuf.at[slot, src, pl.ds(pl.multiple_of(edge_src, TILE), TILE), :],
            dst_ref=ubuf.at[slot, dst, pl.ds(pl.multiple_of(edge_dst, TILE), TILE), :],
            send_sem=sc.at[slot, way],
            recv_sem=rc.at[slot, way],
            device_id=(grp, to, other),
            device_id_type=MESH,
        )

    def copy_y(slot):
        return pltpu.make_async_remote_copy(
            src_ref=ubuf.at[slot, pl.ds(1, depth), pl.ds(pl.multiple_of(edge_src, TILE), TILE), :],
            dst_ref=ubuf.at[slot, pl.ds(1, depth), pl.ds(pl.multiple_of(edge_dst, TILE), TILE), :],
            send_sem=sy.at[slot],
            recv_sem=ry.at[slot],
            device_id=(grp, slab, other),
            device_id_type=MESH,
        )

    def both(do_up, do_dn):
        pl.when(has_up)(do_up)
        pl.when(has_dn)(do_dn)

    def send_z(slot, step):
        both(lambda: copy_z(slot, 0, step).start(), lambda: copy_z(slot, 1, step).start())

    def send_c(slot):
        both(lambda: copy_c(slot, 0).start(), lambda: copy_c(slot, 1).start())

    def recv_z(slot, step):
        both(lambda: copy_z(slot, 1, step).wait_recv(), lambda: copy_z(slot, 0, step).wait_recv())

    def recv_c(slot):
        both(lambda: copy_c(slot, 1).wait_recv(), lambda: copy_c(slot, 0).wait_recv())

    peers = 1 + 2 * has_up.astype(jnp.int32) + 2 * has_dn.astype(jnp.int32)
    pl.semaphore_wait(barrier, peers)

    load_u.wait()
    send_z(0, 0)
    send_c(0)
    copy_y(0).start()

    def initial(step, c):
        send_z(0, step)
        return c

    lax.fori_loop(1, tiles, initial, 0)
    load_g.wait()

    lane = iota2((TILE, width), 1)

    def left(f):
        return jnp.where(lane == 0, 0.0, pltpu.roll(f, 1, 1))

    def right(f):
        return jnp.where(lane == width - 1, 0.0, pltpu.roll(f, width - 1, 1))

    def layer(k, z, r):
        base = pl.multiple_of(TILE * r, TILE)
        here = pl.ds(base, TILE)
        tall = pl.ds(base, 3 * TILE)
        below = ubuf[k, z, tall, :]
        mid = ubuf[k, z + 1, tall, :]
        above = ubuf[k, z + 2, tall, :]
        odd = above - below
        centre = mid[TILE : 2 * TILE]
        odd0 = odd[TILE : 2 * TILE]
        north = mid[TILE + 1 : 2 * TILE + 1]
        south = mid[TILE - 1 : 2 * TILE - 1]
        slope = north - south
        twice = 2.0 * centre
        total = coeff[0, here, :] * (
            above[TILE : 2 * TILE] + below[TILE : 2 * TILE] - twice
        )
        total = total + coeff[1, here, :] * (north + south - twice)
        total = total + coeff[2, here, :] * (right(centre) + left(centre) - twice)
        total = total + coeff[3, here, :] * (
            odd[TILE + 1 : 2 * TILE + 1] - odd[TILE - 1 : 2 * TILE - 1]
        )
        total = total + coeff[4, here, :] * (right(odd0) - left(odd0))
        total = total + coeff[5, here, :] * (right(slope) - left(slope))
        dif[...] = total + centre
        up = pl.ds(pl.multiple_of(base + TILE, TILE), TILE)
        for x in range(0, width, CHUNK):
            xs = pl.ds(x, CHUNK)
            du, v2, w2, s2 = ionic(
                ubuf[k, z + 1, up, xs], out[1, z, here, xs], out[2, z, here, xs],
                out[3, z, here, xs],
            )
            u2 = dif[:, xs] + du
            ubuf[k + 1, z + 1, up, xs] = u2
            out[0, z, here, xs] = u2
            out[1, z, here, xs] = v2
            out[2, z, here, xs] = w2
            out[3, z, here, xs] = s2

    def chunk(n, c):
        k = n // tiles
        step = n % tiles
        r = row_of(step)

        @pl.when(step == 0)
        def _():
            recv_z(k, 0)
            copy_y(k).wait_recv()
            recv_c(k)

        @pl.when(step < tiles - 1)
        def _():
            recv_z(k, step + 1)

        def outer(m, c):
            layer(k, m * (depth - 1), r)
            return c

        lax.fori_loop(0, 2, outer, 0)

        @pl.when(k < SUB - 1)
        def _():
            send_z(k + 1, step)

            @pl.when(step == 0)
            def _():
                send_c(k + 1)

        def inner(m, c):
            layer(k, m, r)
            return c

        lax.fori_loop(1, depth - 1, inner, 0)

        @pl.when((k < SUB - 1) & (step == 0))
        def _():
            copy_y(k + 1).start()

        return c

    lax.fori_loop(0, SUB * tiles, chunk, 0)

    pair_x = (iota2((256, 128), 0) // 2 == iota2((256, 128), 1)).astype(F32)
    half = rows // 2
    pair_y = (iota2((half, rows), 0) == iota2((half, rows), 1) // 2).astype(F32)
    pair_y2 = (iota2((half // 2, half), 0) == iota2((half // 2, half), 1) // 2).astype(F32)
    for h in range(width // 256):
        for q in range(depth // 2):
            xs = slice(h * 256, (h + 1) * 256)
            layers = out[0, 2 * q, :, xs] + out[0, 2 * q + 1, :, xs]
            mean = jnp.dot(layers, pair_x, precision=HI, preferred_element_type=F32)
            mean = 0.125 * jnp.dot(pair_y, mean, precision=HI, preferred_element_type=F32)
            xo = slice(h * 128, (h + 1) * 128)
            before = tension[q, :, xo]
            ten_out[q, :, xo] = before + 0.5 * (mean - before)
    for h in range(width // 512):
        xs = slice(h * 256, (h + 1) * 256)
        layers = ten_out[0, :, xs] + ten_out[1, :, xs]
        mean = jnp.dot(layers, pair_x, precision=HI, preferred_element_type=F32)
        mean = 0.125 * jnp.dot(pair_y2, mean, precision=HI, preferred_element_type=F32)
        act_out[0, :, h * 128 : (h + 1) * 128] = mean

    copy_y(0).wait_send()

    def drain(slot, c):
        both(lambda: copy_c(slot, 0).wait_send(), lambda: copy_c(slot, 1).wait_send())

        @pl.when(slot > 0)
        def _():
            copy_y(slot).wait_send()

        def tile(step, c):
            both(
                lambda: copy_z(slot, 0, step).wait_send(),
                lambda: copy_z(slot, 1, step).wait_send(),
            )
            return c

        return lax.fori_loop(0, tiles, tile, c)

    lax.fori_loop(0, SUB, drain, 0)


def excite(slabs, states, cond, tension):
    _, depth, rows, width = states.shape
    tiles = rows // TILE
    vmem = pl.BlockSpec(memory_space=pltpu.VMEM)
    dma = pltpu.SemaphoreType.DMA
    return pl.pallas_call(
        functools.partial(excite_kernel, slabs),
        out_shape=(
            jax.ShapeDtypeStruct(states.shape, F32),
            jax.ShapeDtypeStruct(tension.shape, F32),
            jax.ShapeDtypeStruct(cond.shape[1:], F32),
        ),
        in_specs=[pl.BlockSpec(memory_space=pl.ANY), vmem, vmem],
        out_specs=(vmem, vmem, vmem),
        scratch_shapes=[
            pltpu.VMEM((SUB + 1, depth + 2, rows + 2 * TILE, width), F32),
            pltpu.VMEM((6, rows, width), F32),
            pltpu.VMEM((TILE, width), F32),
            dma((2,)),
            dma((SUB, 2, tiles)),
            dma((SUB, 2, tiles)),
            dma((SUB, 2)),
            dma((SUB, 2)),
            dma((SUB,)),
            dma((SUB,)),
        ],
        compiler_params=pltpu.CompilerParams(
            collective_id=0, has_side_effects=True, vmem_limit_bytes=40 << 20
        ),
        cost_estimate=pl.CostEstimate(
            flops=200_000_000, bytes_accessed=16 << 20, transcendentals=6_000_000
        ),
        name="excite",
    )(states, cond, tension)


def first_piola(f, active, fdir):
    second = {}
    for a in range(3):
        for b in range(a, 3):
            right = f[0][a] * f[0][b] + f[1][a] * f[1][b] + f[2][a] * f[2][b]
            second[a, b] = 0.5 * (right - (1.0 if a == b else 0.0))
    trace = second[0, 0] + second[1, 1] + second[2, 2]
    pull = 0.5 * active
    for a in range(3):
        scaled = pull * fdir[a]
        for b in range(a, 3):
            second[a, b] = second[a, b] + scaled * fdir[b]
        second[a, a] = second[a, a] + trace
    for a in range(3):
        for b in range(a):
            second[a, b] = second[b, a]
    return [
        f[i][0] * second[0, a] + f[i][1] * second[1, a] + f[i][2] * second[2, a]
        for a in range(3)
        for i in range(3)
    ]


def metric(f, fdir):
    cof = [[None] * 3 for _ in range(3)]
    for i in range(3):
        for j in range(3):
            cof[i][j] = (
                f[(i + 1) % 3][(j + 1) % 3] * f[(i + 2) % 3][(j + 2) % 3]
                - f[(i + 1) % 3][(j + 2) % 3] * f[(i + 2) % 3][(j + 1) % 3]
            )
    det = f[0][0] * cof[0][0] + f[0][1] * cof[0][1] + f[0][2] * cof[0][2]
    scale = 1.0 / det
    inverse = [[cof[i][j] * scale for i in range(3)] for j in range(3)]
    g = [inverse[a][0] * fdir[0] + inverse[a][1] * fdir[1] + inverse[a][2] * fdir[2] for a in range(3)]
    comps = []
    for a, b in PAIRS:
        inner = (
            inverse[a][0] * inverse[b][0]
            + inverse[a][1] * inverse[b][1]
            + inverse[a][2] * inverse[b][2]
        )
        comps.append(SIGMA_TRANS * inner + (SIGMA_LONG - SIGMA_TRANS) * (g[a] * g[b]))
    return comps


RADIUS = 2 * MECH_STEPS + 1


def mech_kernel(slabs, where, fixed, active, disp_out, cond_out, win, stress):
    slab = where[0]
    rows, width = active.shape[2], active.shape[3]
    lane = iota2((rows, width), 1)
    line = iota2((rows, width), 0)

    def left(f):
        return jnp.where(lane == 0, 0.0, pltpu.roll(f, 1, 1))

    def right(f):
        return jnp.where(lane == width - 1, 0.0, pltpu.roll(f, width - 1, 1))

    def south(f):
        return jnp.where(line == 0, 0.0, pltpu.roll(f, 1, 0))

    def north(f):
        return jnp.where(line == rows - 1, 0.0, pltpu.roll(f, rows - 1, 0))

    def sx(f):
        return 0.125 * (left(f) + right(f)) + 0.75 * f

    def dx(f):
        return 0.5 * (right(f) - left(f))

    def sy(f):
        return 0.125 * (south(f) + north(f)) + 0.75 * f

    def dy(f):
        return 0.5 * (north(f) - south(f))

    def inside(j):
        zz = slab + j - RADIUS
        return (zz >= 0) & (zz < slabs), jnp.clip(zz, 0, slabs - 1)

    def fill(j, c):
        ok, zz = inside(j)
        for i in range(3):
            win[i, j] = jnp.where(ok, fixed[i, zz], 0.0)
        return c

    lax.fori_loop(0, 2 * RADIUS + 1, fill, 0)

    def deformation(j):
        f = []
        for i in range(3):
            low, mid, high = win[i, j - 1], win[i, j], win[i, j + 1]
            zs = 0.125 * (low + high) + 0.75 * mid
            zd = 0.5 * (high - low)
            f.append([sy(sx(zd)), dy(sx(zs)), sy(dx(zs))])
            f[i][i] = f[i][i] + 1.0
        return f

    def directions(zz):
        return [fixed[3 + a, zz] for a in range(3)]

    def stresses(j, c):
        ok, zz = inside(j)
        pieces = first_piola(deformation(j), active[0, zz], directions(zz))
        for n in range(9):
            stress[n, j] = jnp.where(ok, pieces[n], 0.0)
        return c

    def move(j, c):
        ok, _ = inside(j)
        for i in range(3):
            zd = 0.5 * (stress[i, j + 1] - stress[i, j - 1])
            ys = 0.125 * (stress[3 + i, j - 1] + stress[3 + i, j + 1]) + 0.75 * stress[3 + i, j]
            xs = 0.125 * (stress[6 + i, j - 1] + stress[6 + i, j + 1]) + 0.75 * stress[6 + i, j]
            force = sy(sx(zd) + dx(xs)) + dy(sx(ys))
            win[i, j] = jnp.where(ok, win[i, j] + MECH_RATE * force, 0.0)
        return c

    for turn in range(MECH_STEPS):
        reach = RADIUS - 1 - 2 * turn
        lax.fori_loop(RADIUS - reach, RADIUS + reach + 1, stresses, 0)
        reach = reach - 1
        lax.fori_loop(RADIUS - reach, RADIUS + reach + 1, move, 0)

    comps = metric(deformation(RADIUS), directions(slab))
    half = disp_out.shape[2]
    first = where[1] == 0
    for i in range(3):
        whole = win[i, RADIUS]
        disp_out[i, 0] = jnp.where(first, whole[:half], whole[half:])
    for n in range(6):
        cond_out[n, 0] = jnp.where(first, comps[n][:half], comps[n][half:])


def mechanics(slabs, where, fixed, active, rows):
    width = active.shape[3]
    full = active.shape[2]
    vmem = pl.BlockSpec(memory_space=pltpu.VMEM)
    return pl.pallas_call(
        functools.partial(mech_kernel, slabs),
        out_shape=(
            jax.ShapeDtypeStruct((3, 1, rows, width), F32),
            jax.ShapeDtypeStruct((6, 1, rows, width), F32),
        ),
        in_specs=[pl.BlockSpec(memory_space=pltpu.SMEM), vmem, vmem],
        out_specs=(vmem, vmem),
        scratch_shapes=[
            pltpu.VMEM((3, 2 * RADIUS + 1, full, width), F32),
            pltpu.VMEM((9, 2 * RADIUS + 1, full, width), F32),
        ],
        compiler_params=pltpu.CompilerParams(vmem_limit_bytes=40 << 20),
        name="mechanics",
    )(where, fixed, active)


def fiber_dir(fiber):
    index = fiber.astype(F32)
    theta = -1.0 + 2.0 * index / (NFIB - 1)
    tilt = 0.3 * jnp.sin(3.0 * index)
    return jnp.stack(
        [jnp.sin(tilt), jnp.cos(tilt) * jnp.sin(theta), jnp.cos(tilt) * jnp.cos(theta)]
    )


def gathered(field):
    whole = lax.all_gather(field, ("slab", "col"))
    slabs, cols = lax.axis_size("slab"), lax.axis_size("col")
    count, _, rows, width = field.shape
    whole = whole.reshape(slabs, cols, count, rows, width)
    return whole.transpose(2, 0, 1, 3, 4).reshape(count, slabs, cols * rows, width)


def on_device(slabs, states, cond, tension, fiber, disp):
    fixed = gathered(jnp.concatenate([disp, fiber_dir(fiber)]))
    states_next, tension_next, active = excite(slabs, states, cond, tension)
    whole = gathered(active[None])
    where = jnp.stack([lax.axis_index("slab"), lax.axis_index("col")]).astype(jnp.int32)
    disp_next, cond_next = mechanics(slabs, where, fixed, whole, disp.shape[2])
    return states_next, tension_next, disp_next, cond_next


def solution(mesh):
    wide = P(None, ("grp", "slab"), "col", None)
    flat = P(("grp", "slab"), "col", None)
    return jax.shard_map(
        functools.partial(on_device, mesh.shape["slab"]),
        mesh=mesh,
        in_specs=(wide, wide, flat, flat, wide),
        out_specs=(wide, flat, wide, wide),
        check_vma=False,
    )
```

time: 315 us -> 127 us (0.40)
  starting transfers between devices: 97.6 us -> 0.04 us
  local copies, waits for them, and re-layouts: 88.1 us -> 10.3 us
  Pallas kernels: 0 us -> 72.8 us
  other arithmetic: 71.7 us -> 2.43 us
  waiting for transfers between devices: 53.7 us -> 0.02 us
  blocking collectives: 0 us -> 26.8 us
  between operations: 1.88 us -> 14.1 us
    ppermute x36 -> x0, starting transfers between devices: 97.6 us -> none  [the longest x18 74.1 us: extended(): before = lax.ppermute(last, axis, up)]
    pallas_call x0 -> x2, Pallas kernels: none -> 72.8 us  [the longest x1 63.4 us: excite(): pl.pallas_call(functools.partial(excite_kernel, slabs), out_shape=(jax.Sh...]
    reshape x1, local copies, waits for them, and re-layouts: 68.4 us -> 1.68 us  [gathered(): whole = whole.reshape(slabs, cols, count, rows, width)]
    ppermute x36 -> x0, waiting for transfers between devices: 53.7 us -> none  [the longest x18 34.7 us: extended(): before = lax.ppermute(last, axis, up)]
    add x31 -> x0, other arithmetic: 33 us -> none  [the longest x4 30.7 us: excite_step(): new_volt = volt + diffusion(padded, coeff) + STEP_TIME * ion]
    all_gather x0 -> x1, blocking collectives: none -> 26.8 us  [gathered(): whole = lax.all_gather(field, ('slab', 'col'))]
    reduce_sum x3 -> x0, other arithmetic: 24.3 us -> none  [coarsen(): return jnp.mean(shaped, axis=(1, 3, 5))]
    broadcast_in_dim x21 -> x0, local copies, waits for them, and re-layouts: 7.03 us -> none  [the longest x9 6.6 us: upsample(): jnp.repeat(jnp.repeat(jnp.repeat(cond, 4, axis=1), 4, axis=2), 4, axis=3)]
  transfers between devices with their start and end apart: 36 -> 1, of which waited for: 19 -> 0; matrix products, arithmetic and copies ran while one was open for 10% -> 0% of each run, Pallas kernels for 0% -> 50%
where the time goes in v1:
time: 127 us
  Pallas kernels  72.8 us (57%)
  blocking collectives  26.8 us (21%)
  between operations  14.1 us (11%)
  local copies, waits for them, and re-layouts  10.3 us (8%)
  other arithmetic  2.43 us (2%)
    pallas_call x1, Pallas kernels, excite(): pl.pallas_call(functools.partial(excite_kernel, slabs), out_shape=(jax.Sh...  63.4 us
    all_gather x1, blocking collectives, gathered(): whole = lax.all_gather(field, ('slab', 'col'))  26.8 us
    pallas_call x1, Pallas kernels, mechanics(): pl.pallas_call(functools.partial(mech_kernel, slabs), out_shape=(jax.Shap...  9.42 us
    unnamed x12, local copies, waits for them, and re-layouts  8.66 us
  transfers between devices with their start and end apart: 1, of which 0 were waited for; matrix products, arithmetic and copies ran while one was open for 0% of the time, Pallas kernels for 50%

profile of v1, /device:TPU:0, one launch (start us, length us, event | category | flops | bytes accessed | tf_op | source)
XLA Modules:
  0.0 126.5 jit_solution(15744081242642421899)
XLA Ops:
  7.2 0.0 all-gather.4.cloned.1.call-start
  7.2 0.9 sine_bitcast_fusion
  8.1 1.4 %pad_maximum_fusion = f32[6,1,16,256]{3,2,1,0:T(8,128)} fusion(f32[1,1,16,256]{3,2,1,0:T(8,128)S(1)} %get-tuple-element.15, f32[1,1,16,256]{3,2,1,0:T(8,128)S(1)} %get-tuple-element.16, f32[1,1,16,256]{3,2,1,0:T(8,128)S(1)} %get-tuple-element.14, f32[3,1,16,256]{3,2,1,0:T(8,128)} %param.9), kind=kLoop, calls=%fused_computation | loop fusion | flops 73728 | bytes 196608 | tf_op jit(solution)/shard_map/concatenate | solution.py:550
  9.6 0.0 all-gather.4.cloned.1.call-update
  9.6 0.0 copy-start.2
  9.6 2.2 %copy-done.2 = f32[4,4,64,1024]{3,2,1,0:T(8,128)S(1)} copy-done((f32[4,4,64,1024]{3,2,1,0:T(8,128)S(1)}, f32[4,4,64,1024]{3,2,1,0:T(8,128)}, u32[]{:S(2)}) %copy-start.2) | copy-done | bytes 4194328
  11.8 0.0 copy-start.3
  11.8 0.9 copy-done.3
  12.7 0.0 copy-start.4
  12.7 0.9 copy-done.4
  13.6 63.4 %excite.1 = (f32[4,4,64,1024]{3,2,1,0:T(8,128)S(1)}, f32[2,32,512]{2,1,0:T(8,128)S(1)}, f32[1,16,256]{2,1,0:T(8,128)S(1)}) custom-call(f32[4,4,64,1024]{3,2,1,0:T(8,128)S(1)} %copy-done.2, f32[6,1,16,256]{3,2,1,0:T(8,128)S(1)} %copy-done.4, f32[2,32,512]{2,1,0:T(8,128)S(1)} %copy-done.3), custom_call_target="tpu_custom_call" | custom-call | flops 200000000 | bytes 16777216 | tf_op jit(solution)/shard_map/excite/pallas_call | solution.py:343
  77.0 0.0 copy-start
  77.0 2.0 %copy-done = f32[4,4,64,1024]{3,2,1,0:T(8,128)} copy-done((f32[4,4,64,1024]{3,2,1,0:T(8,128)}, f32[4,4,64,1024]{3,2,1,0:T(8,128)S(1)}, u32[]{:S(2)}) %copy-start) | copy-done | bytes 4194328
  79.0 0.1 pad_add_fusion.where
  79.1 26.8 %all-gather.1 = f32[16,16,256]{2,1,0:T(8,128)S(1)} all-gather(f32[1,16,256]{2,1,0:T(8,128)S(1)} %get-tuple-element.11), channel_id=3, replica_groups=mesh['grp'=2,'slab'=8,'col'=2] {'slab','col'}, dimensions={0}, use_global_device_ids=true | all-gather | bytes 278528 | tf_op jit(solution)/shard_map/all_gather | solution.py:542
  105.9 0.0 all-gather.4.cloned.1.call-done
  105.9 0.0 copy-start.1
  105.9 1.7 %copy.10 = f32[8,2,6,16,256]{4,3,1,0,2:T(8,128)S(1)} copy(f32[8,2,6,16,256]{4,3,2,1,0:T(8,128)} %bitcast.15) | data formatting | bytes 3145728 | tf_op jit(solution)/shard_map/reshape | solution.py:545
  107.6 9.4 %mechanics.1 = (f32[3,1,16,256]{3,2,1,0:T(8,128)}, f32[6,1,16,256]{3,2,1,0:T(8,128)}) custom-call(s32[2]{0:T(128)S(1)} %pad_add_fusion.where, f32[6,8,32,256]{3,2,1,0:T(8,128)S(1)} %bitcast.13, f32[1,8,32,256]{3,2,1,0:T(8,128)S(1)} %bitcast.14), custom_call_target="tpu_custom_call" | custom-call | tf_op jit(solution)/shard_map/mechanics/pallas_call | solution.py:515
  117.0 0.0 copy-done.1
  117.0 2.0 %copy.13 = f32[4,4,64,1024]{3,2,1,0:T(8,128)} copy(f32[4,4,64,1024]{3,2,1,0:T(8,128)S(1)} %copy-done.1) | data formatting | bytes 8388608
  119.0 0.7 copy.14
Async XLA Ops:
  7.2 98.7 %all-gather.4.cloned.1.call-start = ((), (), s32[]{:S(2)}) async-start(), calls=%async_computation | async-start | bytes 1671168 | tf_op jit(solution)/shard_map/all_gather | solution.py:542
  9.6 2.2 %copy-start.2 = (f32[4,4,64,1024]{3,2,1,0:T(8,128)S(1)}, f32[4,4,64,1024]{3,2,1,0:T(8,128)}, u32[]{:S(2)}) copy-start(f32[4,4,64,1024]{3,2,1,0:T(8,128)} %states.1) | copy-start | bytes 12582916
  11.8 0.9 copy-start.3
  12.7 0.9 copy-start.4
  77.0 2.0 %copy-start = (f32[4,4,64,1024]{3,2,1,0:T(8,128)}, f32[4,4,64,1024]{3,2,1,0:T(8,128)S(1)}, u32[]{:S(2)}) copy-start(f32[4,4,64,1024]{3,2,1,0:T(8,128)S(1)} %get-tuple-element.21) | copy-start | bytes 12582916
  105.9 11.1 %copy-start.1 = (f32[4,4,64,1024]{3,2,1,0:T(8,128)S(1)}, f32[4,4,64,1024]{3,2,1,0:T(8,128)}, u32[]{:S(2)}) copy-start(f32[4,4,64,1024]{3,2,1,0:T(8,128)} %copy-done) | copy-start | bytes 12582916
Sparse Core Ops, SparseCore 0:
  10.9 55.8 all-gather.3

commit v2 on v1

--- a/solution.py
+++ b/solution.py
@@ -20,6 +20,8 @@
 F32 = jnp.float32
 TILE = 8
 CHUNK = 256
+RADIUS = 2 * MECH_STEPS + 1
+REACH = RADIUS - 1
 
 
 def ionic(u, v, w, s):
@@ -57,8 +59,9 @@
 
 
 def excite_kernel(
-    slabs, states, cond, tension, out, ten_out, act_out,
-    ubuf, coeff, dif, load_sem, sz, rz, sc, rc, sy, ry,
+    slabs, states, cond_hbm, ten_hbm, out_hbm, ten_out, act_out,
+    ubuf, out, cond, tension, coeff, dif, act_win,
+    load_sem, store_sem, sz, rz, sc, rc, sy, ry, sa, ra,
 ):
     grp = lax.axis_index("grp")
     slab = lax.axis_index("slab")
@@ -77,25 +80,32 @@
     load_g = pltpu.make_async_copy(
         states.at[pl.ds(1, 3)], out.at[pl.ds(1, 3)], load_sem.at[1]
     )
+    load_c = pltpu.make_async_copy(cond_hbm, cond, load_sem.at[2])
+    load_t = pltpu.make_async_copy(ten_hbm, tension, load_sem.at[3])
     load_u.start()
+    load_c.start()
     load_g.start()
+    load_t.start()
 
     barrier = pltpu.get_barrier_semaphore()
 
     def greet(where):
         pl.semaphore_signal(barrier, inc=1, device_id=where, device_id_type=MESH)
 
-    greet((grp, slab, other))
-
-    @pl.when(has_up)
-    def _():
-        greet((grp, slab + 1, col))
-        greet((grp, slab + 1, other))
-
-    @pl.when(has_dn)
-    def _():
-        greet((grp, slab - 1, col))
-        greet((grp, slab - 1, other))
+    peers = -1
+    for d in range(-REACH, REACH + 1):
+        valid = (slab + d >= 0) & (slab + d < slabs)
+        peers = peers + 2 * valid.astype(jnp.int32)
+
+        @pl.when(valid)
+        def _(d=d):
+            greet((grp, slab + d, other))
+            if d != 0:
+                greet((grp, slab + d, col))
+
+        @pl.when(jnp.logical_not(valid))
+        def _(d=d):
+            act_win[d + REACH] = jnp.zeros(act_win.shape[1:], F32)
 
     blank = jnp.zeros((TILE, width), F32)
 
@@ -121,17 +131,6 @@
     @pl.when(slab == slabs - 1)
     def _():
         clear_z(depth + 1)
-
-    spread_x = (iota2((128, 512), 0) == iota2((128, 512), 1) // 4).astype(F32)
-    spread_y = (iota2((rows, rows // 4), 0) // 4 == iota2((rows, rows // 4), 1)).astype(F32)
-    for c in range(6):
-        for h in range(width // 512):
-            part = jnp.dot(
-                cond[c, 0, :, h * 128 : (h + 1) * 128], spread_x, precision=HI,
-                preferred_element_type=F32,
-            )
-            part = jnp.dot(spread_y, part, precision=HI, preferred_element_type=F32)
-            coeff[c, :, h * 512 : (h + 1) * 512] = part if c < 3 else 0.5 * part
 
     def row_of(step):
         return jnp.where(col == 1, step, tiles - 1 - step)
@@ -151,15 +150,13 @@
         )
 
     def copy_c(slot, way):
-        src = depth if way == 0 else 1
-        dst = 0 if way == 0 else depth + 1
-        to = slab + 1 if way == 0 else slab - 1
+        at = depth + 1 if way == 0 else 0
         return pltpu.make_async_remote_copy(
-            src_ref=ubuf.at[slot, src, pl.ds(pl.multiple_of(edge_src, TILE), TILE), :],
-            dst_ref=ubuf.at[slot, dst, pl.ds(pl.multiple_of(edge_dst, TILE), TILE), :],
+            src_ref=ubuf.at[slot, at, pl.ds(pl.multiple_of(edge_src, TILE), TILE), :],
+            dst_ref=ubuf.at[slot, at, pl.ds(pl.multiple_of(edge_dst, TILE), TILE), :],
             send_sem=sc.at[slot, way],
             recv_sem=rc.at[slot, way],
-            device_id=(grp, to, other),
+            device_id=(grp, slab, other),
             device_id_type=MESH,
         )
 
@@ -187,14 +184,12 @@
         both(lambda: copy_z(slot, 1, step).wait_recv(), lambda: copy_z(slot, 0, step).wait_recv())
 
     def recv_c(slot):
-        both(lambda: copy_c(slot, 1).wait_recv(), lambda: copy_c(slot, 0).wait_recv())
-
-    peers = 1 + 2 * has_up.astype(jnp.int32) + 2 * has_dn.astype(jnp.int32)
+        both(lambda: copy_c(slot, 0).wait_recv(), lambda: copy_c(slot, 1).wait_recv())
+
     pl.semaphore_wait(barrier, peers)
 
     load_u.wait()
     send_z(0, 0)
-    send_c(0)
     copy_y(0).start()
 
     def initial(step, c):
@@ -202,6 +197,19 @@
         return c
 
     lax.fori_loop(1, tiles, initial, 0)
+    load_c.wait()
+
+    spread_x = (iota2((128, 512), 0) == iota2((128, 512), 1) // 4).astype(F32)
+    spread_y = (iota2((rows, rows // 4), 0) // 4 == iota2((rows, rows // 4), 1)).astype(F32)
+    for c in range(6):
+        for h in range(width // 512):
+            part = jnp.dot(
+                cond[c, 0, :, h * 128 : (h + 1) * 128], spread_x, precision=HI,
+                preferred_element_type=F32,
+            )
+            part = jnp.dot(spread_y, part, precision=HI, preferred_element_type=F32)
+            coeff[c, :, h * 512 : (h + 1) * 512] = part if c < 3 else 0.5 * part
+
     load_g.wait()
 
     lane = iota2((TILE, width), 1)
@@ -251,6 +259,12 @@
             out[2, z, here, xs] = w2
             out[3, z, here, xs] = s2
 
+    def leave(step):
+        at = pl.ds(pl.multiple_of(TILE * row_of(step), TILE), TILE)
+        return pltpu.make_async_copy(
+            out.at[:, :, at, :], out_hbm.at[:, :, at, :], store_sem.at[step]
+        )
+
     def chunk(n, c):
         k = n // tiles
         step = n % tiles
@@ -259,13 +273,17 @@
         @pl.when(step == 0)
         def _():
             recv_z(k, 0)
-            copy_y(k).wait_recv()
-            recv_c(k)
+            send_c(k)
 
         @pl.when(step < tiles - 1)
         def _():
             recv_z(k, step + 1)
 
+        @pl.when(step == 0)
+        def _():
+            copy_y(k).wait_recv()
+            recv_c(k)
+
         def outer(m, c):
             layer(k, m * (depth - 1), r)
             return c
@@ -276,10 +294,6 @@
         def _():
             send_z(k + 1, step)
 
-            @pl.when(step == 0)
-            def _():
-                send_c(k + 1)
-
         def inner(m, c):
             layer(k, m, r)
             return c
@@ -290,9 +304,15 @@
         def _():
             copy_y(k + 1).start()
 
+        @pl.when(k == SUB - 1)
+        def _():
+            leave(step).start()
+
         return c
 
     lax.fori_loop(0, SUB * tiles, chunk, 0)
+
+    load_t.wait()
 
     pair_x = (iota2((256, 128), 0) // 2 == iota2((256, 128), 1)).astype(F32)
     half = rows // 2
@@ -312,7 +332,38 @@
         layers = ten_out[0, :, xs] + ten_out[1, :, xs]
         mean = jnp.dot(layers, pair_x, precision=HI, preferred_element_type=F32)
         mean = 0.125 * jnp.dot(pair_y2, mean, precision=HI, preferred_element_type=F32)
-        act_out[0, :, h * 128 : (h + 1) * 128] = mean
+        act_win[REACH, col, :, h * 128 : (h + 1) * 128] = mean
+
+    def copy_a(d, to):
+        return pltpu.make_async_remote_copy(
+            src_ref=act_win.at[REACH, col],
+            dst_ref=act_win.at[REACH - d, col],
+            send_sem=sa.at[d + REACH, 0 if to is other else 1],
+            recv_sem=ra.at[REACH - d, 0 if to is other else 1],
+            device_id=(grp, slab + d, to),
+            device_id_type=MESH,
+        )
+
+    def come_a(d, to):
+        return pltpu.make_async_remote_copy(
+            src_ref=act_win.at[REACH, col],
+            dst_ref=act_win.at[REACH + d, to],
+            send_sem=sa.at[d + REACH, 0 if to is other else 1],
+            recv_sem=ra.at[REACH + d, 0 if to is other else 1],
+            device_id=(grp, slab + d, to),
+            device_id_type=MESH,
+        )
+
+    def each_a(act):
+        for d in sorted(range(-REACH, REACH + 1), key=lambda d: -abs(d)):
+
+            @pl.when((slab + d >= 0) & (slab + d < slabs))
+            def _(d=d):
+                act(d, other)
+                if d != 0:
+                    act(d, col)
+
+    each_a(lambda d, to: copy_a(d, to).start())
 
     copy_y(0).wait_send()
 
@@ -334,35 +385,53 @@
 
     lax.fori_loop(0, SUB, drain, 0)
 
+    def left_all(step, c):
+        leave(step).wait()
+        return c
+
+    lax.fori_loop(0, tiles, left_all, 0)
+    each_a(lambda d, to: copy_a(d, to).wait_send())
+    each_a(lambda d, to: come_a(d, to).wait_recv())
+    act_out[...] = act_win[...]
+
 
 def excite(slabs, states, cond, tension):
     _, depth, rows, width = states.shape
     tiles = rows // TILE
     vmem = pl.BlockSpec(memory_space=pltpu.VMEM)
+    hbm = pl.BlockSpec(memory_space=pltpu.HBM)
+    window = (2 * REACH + 1, 2, *cond.shape[2:])
     dma = pltpu.SemaphoreType.DMA
     return pl.pallas_call(
         functools.partial(excite_kernel, slabs),
         out_shape=(
             jax.ShapeDtypeStruct(states.shape, F32),
             jax.ShapeDtypeStruct(tension.shape, F32),
-            jax.ShapeDtypeStruct(cond.shape[1:], F32),
+            jax.ShapeDtypeStruct(window, F32),
         ),
-        in_specs=[pl.BlockSpec(memory_space=pl.ANY), vmem, vmem],
-        out_specs=(vmem, vmem, vmem),
+        in_specs=[hbm, hbm, hbm],
+        out_specs=(hbm, vmem, vmem),
         scratch_shapes=[
             pltpu.VMEM((SUB + 1, depth + 2, rows + 2 * TILE, width), F32),
+            pltpu.VMEM(states.shape, F32),
+            pltpu.VMEM(cond.shape, F32),
+            pltpu.VMEM(tension.shape, F32),
             pltpu.VMEM((6, rows, width), F32),
             pltpu.VMEM((TILE, width), F32),
-            dma((2,)),
+            pltpu.VMEM(window, F32),
+            dma((4,)),
+            dma((tiles,)),
             dma((SUB, 2, tiles)),
             dma((SUB, 2, tiles)),
             dma((SUB, 2)),
             dma((SUB, 2)),
             dma((SUB,)),
             dma((SUB,)),
+            dma((2 * REACH + 1, 2)),
+            dma((2 * REACH + 1, 2)),
         ],
         compiler_params=pltpu.CompilerParams(
-            collective_id=0, has_side_effects=True, vmem_limit_bytes=40 << 20
+            collective_id=0, has_side_effects=True, vmem_limit_bytes=61 << 20
         ),
         cost_estimate=pl.CostEstimate(
             flops=200_000_000, bytes_accessed=16 << 20, transcendentals=6_000_000
@@ -417,12 +486,15 @@
     return comps
 
 
-RADIUS = 2 * MECH_STEPS + 1
-
-
-def mech_kernel(slabs, where, fixed, active, disp_out, cond_out, win, stress):
+def mech_kernel(
+    slabs, where, fixed, active, ten_in, states_in,
+    disp_out, cond_out, ten_out, states_out, win, stress, sem,
+):
     slab = where[0]
-    rows, width = active.shape[2], active.shape[3]
+    rows, width = 2 * active.shape[2], active.shape[3]
+    hand_on = pltpu.make_async_copy(states_in, states_out, sem)
+    hand_on.start()
+    ten_out[...] = ten_in[...]
     lane = iota2((rows, width), 1)
     line = iota2((rows, width), 0)
 
@@ -454,10 +526,13 @@
         zz = slab + j - RADIUS
         return (zz >= 0) & (zz < slabs), jnp.clip(zz, 0, slabs - 1)
 
+    def joined(zz, n):
+        return jnp.concatenate([fixed[2 * zz, n], fixed[2 * zz + 1, n]], axis=0)
+
     def fill(j, c):
         ok, zz = inside(j)
         for i in range(3):
-            win[i, j] = jnp.where(ok, fixed[i, zz], 0.0)
+            win[i, j] = jnp.where(ok, joined(zz, i), 0.0)
         return c
 
     lax.fori_loop(0, 2 * RADIUS + 1, fill, 0)
@@ -473,11 +548,12 @@
         return f
 
     def directions(zz):
-        return [fixed[3 + a, zz] for a in range(3)]
+        return [joined(zz, 3 + a) for a in range(3)]
 
     def stresses(j, c):
         ok, zz = inside(j)
-        pieces = first_piola(deformation(j), active[0, zz], directions(zz))
+        act = jnp.concatenate([active[j - 1, 0], active[j - 1, 1]], axis=0)
+        pieces = first_piola(deformation(j), act, directions(zz))
         for n in range(9):
             stress[n, j] = jnp.where(ok, pieces[n], 0.0)
         return c
@@ -506,27 +582,32 @@
         disp_out[i, 0] = jnp.where(first, whole[:half], whole[half:])
     for n in range(6):
         cond_out[n, 0] = jnp.where(first, comps[n][:half], comps[n][half:])
-
-
-def mechanics(slabs, where, fixed, active, rows):
-    width = active.shape[3]
-    full = active.shape[2]
+    hand_on.wait()
+
+
+def mechanics(slabs, where, fixed, active, tension, states):
+    _, cols, rows, width = active.shape
+    full = cols * rows
     vmem = pl.BlockSpec(memory_space=pltpu.VMEM)
+    hbm = pl.BlockSpec(memory_space=pltpu.HBM)
     return pl.pallas_call(
         functools.partial(mech_kernel, slabs),
         out_shape=(
             jax.ShapeDtypeStruct((3, 1, rows, width), F32),
             jax.ShapeDtypeStruct((6, 1, rows, width), F32),
+            jax.ShapeDtypeStruct(tension.shape, F32),
+            jax.ShapeDtypeStruct(states.shape, F32),
         ),
-        in_specs=[pl.BlockSpec(memory_space=pltpu.SMEM), vmem, vmem],
-        out_specs=(vmem, vmem),
+        in_specs=[pl.BlockSpec(memory_space=pltpu.SMEM), vmem, vmem, vmem, hbm],
+        out_specs=(vmem, vmem, vmem, hbm),
         scratch_shapes=[
             pltpu.VMEM((3, 2 * RADIUS + 1, full, width), F32),
             pltpu.VMEM((9, 2 * RADIUS + 1, full, width), F32),
+            pltpu.SemaphoreType.DMA,
         ],
-        compiler_params=pltpu.CompilerParams(vmem_limit_bytes=40 << 20),
+        compiler_params=pltpu.CompilerParams(vmem_limit_bytes=61 << 20),
         name="mechanics",
-    )(where, fixed, active)
+    )(where, fixed, active, tension, states)
 
 
 def fiber_dir(fiber):
@@ -538,20 +619,14 @@
     )
 
 
-def gathered(field):
-    whole = lax.all_gather(field, ("slab", "col"))
-    slabs, cols = lax.axis_size("slab"), lax.axis_size("col")
-    count, _, rows, width = field.shape
-    whole = whole.reshape(slabs, cols, count, rows, width)
-    return whole.transpose(2, 0, 1, 3, 4).reshape(count, slabs, cols * rows, width)
-
-
 def on_device(slabs, states, cond, tension, fiber, disp):
-    fixed = gathered(jnp.concatenate([disp, fiber_dir(fiber)]))
+    fixed = jnp.concatenate([disp, fiber_dir(fiber)])
+    fixed = lax.all_gather(fixed[:, 0], ("slab", "col"))
     states_next, tension_next, active = excite(slabs, states, cond, tension)
-    whole = gathered(active[None])
     where = jnp.stack([lax.axis_index("slab"), lax.axis_index("col")]).astype(jnp.int32)
-    disp_next, cond_next = mechanics(slabs, where, fixed, whole, disp.shape[2])
+    disp_next, cond_next, tension_next, states_next = mechanics(
+        slabs, where, fixed, active, tension_next, states_next
+    )
     return states_next, tension_next, disp_next, cond_next
 
 

time: 127 us -> 216 us (1.70)
  Pallas kernels: 72.8 us -> 199 us
  blocking collectives: 26.8 us -> 0 us
  local copies, waits for them, and re-layouts: 10.3 us -> 0 us
    pallas_call x1, Pallas kernels: 9.42 us -> 130 us  [mechanics(): pl.pallas_call(functools.partial(mech_kernel, slabs), out_shape=(jax.Shap...]
    all_gather x1 -> x0, blocking collectives: 26.8 us -> none  [gathered(): whole = lax.all_gather(field, ('slab', 'col'))]
    unnamed x12 -> x0, local copies, waits for them, and re-layouts: 8.66 us -> none
    pallas_call x1, Pallas kernels: 63.4 us -> 68.2 us  [excite(): pl.pallas_call(functools.partial(excite_kernel, slabs), out_shape=(jax.Sh...]
  transfers between devices with their start and end apart: 1 -> 1, of which waited for: 0 -> 0; matrix products, arithmetic and copies ran while one was open for 0% -> 0% of each run, Pallas kernels for 50% -> 32%
where the time goes in v2:
time: 216 us
  Pallas kernels  199 us (92%)
  between operations  14.1 us (7%)
  other arithmetic  2.95 us (1%)
    pallas_call x1, Pallas kernels, mechanics(): pl.pallas_call(functools.partial(mech_kernel, slabs), out_shape=(jax.Shap...  130 us
    pallas_call x1, Pallas kernels, excite(): pl.pallas_call(functools.partial(excite_kernel, slabs), out_shape=(jax.Sh...  68.2 us
  transfers between devices with their start and end apart: 1, of which 0 were waited for; matrix products, arithmetic and copies ran while one was open for 0% of the time, Pallas kernels for 32%

profile of v2, /device:TPU:0, one launch (start us, length us, event | category | flops | bytes accessed | tf_op | source)
XLA Modules:
  0.0 215.7 jit_solution(3968583745454174951)
XLA Ops:
  7.2 0.0 all-gather.3.cloned.1.call-start
  7.2 0.9 sine_bitcast_fusion
  8.1 1.4 pad_maximum_fusion
  9.6 0.0 all-gather.3.cloned.1.call-update
  9.6 68.2 %excite.1 = (f32[4,4,64,1024]{3,2,1,0:T(8,128)}, f32[2,32,512]{2,1,0:T(8,128)}, f32[9,2,16,256]{3,2,1,0:T(8,128)}) custom-call(f32[4,4,64,1024]{3,2,1,0:T(8,128)} %states.1, f32[6,1,16,256]{3,2,1,0:T(8,128)} %cond_hbm.1, f32[2,32,512]{2,1,0:T(8,128)} %ten_hbm.1), custom_call_target="tpu_custom_call" | custom-call | flops 200000000 | bytes 16777216 | tf_op jit(solution)/shard_map/excite/pallas_call | solution.py:405
  77.8 0.6 pad_add_fusion.where
  78.4 0.0 all-gather.3.cloned.1.call-done
  78.4 130.4 %mechanics.1 = (f32[3,1,16,256]{3,2,1,0:T(8,128)}, f32[6,1,16,256]{3,2,1,0:T(8,128)}, f32[2,32,512]{2,1,0:T(8,128)}, f32[4,4,64,1024]{3,2,1,0:T(8,128)}) custom-call(s32[2]{0:T(128)} %pad_add_fusion.where, f32[16,6,16,256]{3,2,1,0:T(8,128)} %bitcast.9, f32[9,2,16,256]{3,2,1,0:T(8,128)} %get-tuple-element.11.active, f32[2,32,512]{2,1,0:T(8,128)} %get-tuple-element.12.ten_in, ...), custom_call_target="tpu_custom_call" | custom-call | tf_op jit(solution)/shard_map/mechanics/pallas_call | solution.py:593
Async XLA Ops:
  7.2 71.3 %all-gather.3.cloned.1.call-start = ((), (), s32[]{:S(2)}) async-start(), calls=%async_computation | async-start | bytes 1671168 | tf_op jit(solution)/shard_map/all_gather | solution.py:624
Sparse Core Ops, SparseCore 0:
  10.9 54.2 all-gather.2

commit v3 on v2

--- a/solution.py
+++ b/solution.py
@@ -211,6 +211,7 @@
             coeff[c, :, h * 512 : (h + 1) * 512] = part if c < 3 else 0.5 * part
 
     load_g.wait()
+    load_t.wait()
 
     lane = iota2((TILE, width), 1)
 
@@ -265,6 +266,26 @@
             out.at[:, :, at, :], out_hbm.at[:, :, at, :], store_sem.at[step]
         )
 
+    pair_x = (iota2((256, 128), 0) // 2 == iota2((256, 128), 1)).astype(F32)
+    pair_y = (iota2((TILE, 2 * TILE), 0) == iota2((TILE, 2 * TILE), 1) // 2).astype(F32)
+    half = rows // 2
+    pair_y2 = (iota2((half // 2, half), 0) == iota2((half // 2, half), 1) // 2).astype(F32)
+
+    def tense(p):
+        fine = pl.ds(pl.multiple_of(2 * TILE * p, 2 * TILE), 2 * TILE)
+        wide = pl.ds(pl.multiple_of(TILE * p, TILE), TILE)
+        for q in range(depth // 2):
+            layers = out[0, 2 * q, fine, :] + out[0, 2 * q + 1, fine, :]
+            pairs = 0.125 * jnp.dot(pair_y, layers, precision=HI, preferred_element_type=F32)
+            for h in range(width // 256):
+                mean = jnp.dot(
+                    pairs[:, h * 256 : (h + 1) * 256], pair_x, precision=HI,
+                    preferred_element_type=F32,
+                )
+                xo = slice(h * 128, (h + 1) * 128)
+                before = tension[q, wide, xo]
+                ten_out[q, wide, xo] = before + 0.5 * (mean - before)
+
     def chunk(n, c):
         k = n // tiles
         step = n % tiles
@@ -308,25 +329,14 @@
         def _():
             leave(step).start()
 
+        @pl.when((k == SUB - 1) & (step % 2 == 1))
+        def _():
+            tense(r // 2)
+
         return c
 
     lax.fori_loop(0, SUB * tiles, chunk, 0)
 
-    load_t.wait()
-
-    pair_x = (iota2((256, 128), 0) // 2 == iota2((256, 128), 1)).astype(F32)
-    half = rows // 2
-    pair_y = (iota2((half, rows), 0) == iota2((half, rows), 1) // 2).astype(F32)
-    pair_y2 = (iota2((half // 2, half), 0) == iota2((half // 2, half), 1) // 2).astype(F32)
-    for h in range(width // 256):
-        for q in range(depth // 2):
-            xs = slice(h * 256, (h + 1) * 256)
-            layers = out[0, 2 * q, :, xs] + out[0, 2 * q + 1, :, xs]
-            mean = jnp.dot(layers, pair_x, precision=HI, preferred_element_type=F32)
-            mean = 0.125 * jnp.dot(pair_y, mean, precision=HI, preferred_element_type=F32)
-            xo = slice(h * 128, (h + 1) * 128)
-            before = tension[q, :, xo]
-            ten_out[q, :, xo] = before + 0.5 * (mean - before)
     for h in range(width // 512):
         xs = slice(h * 256, (h + 1) * 256)
         layers = ten_out[0, :, xs] + ten_out[1, :, xs]
@@ -488,12 +498,15 @@
 
 def mech_kernel(
     slabs, where, fixed, active, ten_in, states_in,
-    disp_out, cond_out, ten_out, states_out, win, stress, sem,
+    disp_out, cond_out, ten_out, states_out, win, stress, held, sem,
 ):
     slab = where[0]
-    rows, width = 2 * active.shape[2], active.shape[3]
-    hand_on = pltpu.make_async_copy(states_in, states_out, sem)
-    hand_on.start()
+    first = where[1] == 0
+    half, width = active.shape[2:]
+    rows = half + TILE
+    fetch = pltpu.make_async_copy(states_in, held, sem.at[0])
+    hand_on = pltpu.make_async_copy(held, states_out, sem.at[1])
+    fetch.start()
     ten_out[...] = ten_in[...]
     lane = iota2((rows, width), 1)
     line = iota2((rows, width), 0)
@@ -526,8 +539,15 @@
         zz = slab + j - RADIUS
         return (zz >= 0) & (zz < slabs), jnp.clip(zz, 0, slabs - 1)
 
+    def beside(a, b):
+        return jnp.where(
+            first,
+            jnp.concatenate([a, b[:TILE]], axis=0),
+            jnp.concatenate([a[half - TILE :], b], axis=0),
+        )
+
     def joined(zz, n):
-        return jnp.concatenate([fixed[2 * zz, n], fixed[2 * zz + 1, n]], axis=0)
+        return beside(fixed[2 * zz, n], fixed[2 * zz + 1, n])
 
     def fill(j, c):
         ok, zz = inside(j)
@@ -552,7 +572,7 @@
 
     def stresses(j, c):
         ok, zz = inside(j)
-        act = jnp.concatenate([active[j - 1, 0], active[j - 1, 1]], axis=0)
+        act = beside(active[j - 1, 0], active[j - 1, 1])
         pieces = first_piola(deformation(j), act, directions(zz))
         for n in range(9):
             stress[n, j] = jnp.where(ok, pieces[n], 0.0)
@@ -571,23 +591,24 @@
     for turn in range(MECH_STEPS):
         reach = RADIUS - 1 - 2 * turn
         lax.fori_loop(RADIUS - reach, RADIUS + reach + 1, stresses, 0)
+        if turn == 0:
+            fetch.wait()
+            hand_on.start()
         reach = reach - 1
         lax.fori_loop(RADIUS - reach, RADIUS + reach + 1, move, 0)
 
     comps = metric(deformation(RADIUS), directions(slab))
-    half = disp_out.shape[2]
-    first = where[1] == 0
     for i in range(3):
         whole = win[i, RADIUS]
-        disp_out[i, 0] = jnp.where(first, whole[:half], whole[half:])
+        disp_out[i, 0] = jnp.where(first, whole[:half], whole[TILE:])
     for n in range(6):
-        cond_out[n, 0] = jnp.where(first, comps[n][:half], comps[n][half:])
+        cond_out[n, 0] = jnp.where(first, comps[n][:half], comps[n][TILE:])
     hand_on.wait()
 
 
 def mechanics(slabs, where, fixed, active, tension, states):
-    _, cols, rows, width = active.shape
-    full = cols * rows
+    _, _, rows, width = active.shape
+    full = rows + TILE
     vmem = pl.BlockSpec(memory_space=pltpu.VMEM)
     hbm = pl.BlockSpec(memory_space=pltpu.HBM)
     return pl.pallas_call(
@@ -603,7 +624,8 @@
         scratch_shapes=[
             pltpu.VMEM((3, 2 * RADIUS + 1, full, width), F32),
             pltpu.VMEM((9, 2 * RADIUS + 1, full, width), F32),
-            pltpu.SemaphoreType.DMA,
+            pltpu.VMEM(states.shape, F32),
+            pltpu.SemaphoreType.DMA((2,)),
         ],
         compiler_params=pltpu.CompilerParams(vmem_limit_bytes=61 << 20),
         name="mechanics",

time: 216 us -> 96.3 us (0.45)
  Pallas kernels: 199 us -> 79 us
    pallas_call x1, Pallas kernels: 130 us -> 9.19 us  [mechanics(): pl.pallas_call(functools.partial(mech_kernel, slabs), out_shape=(jax.Shap...]
  transfers between devices with their start and end apart: 1 -> 1, of which waited for: 0 -> 0; matrix products, arithmetic and copies ran while one was open for 0% -> 1% of each run, Pallas kernels for 32% -> 73%
where the time goes in v3:
time: 96.3 us; the launch traced here: 96.1 us
  Pallas kernels  79 us (82%)
  between operations  14.1 us (15%)
  other arithmetic  2.95 us (3%)
    pallas_call x1, Pallas kernels, excite(): pl.pallas_call(functools.partial(excite_kernel, slabs), out_shape=(jax.Sh...  69.8 us
    pallas_call x1, Pallas kernels, mechanics(): pl.pallas_call(functools.partial(mech_kernel, slabs), out_shape=(jax.Shap...  9.19 us
  transfers between devices with their start and end apart: 1, of which 0 were waited for; matrix products, arithmetic and copies ran while one was open for 1% of the time, Pallas kernels for 73%

profile of v3, /device:TPU:0, one launch (start us, length us, event | category | flops | bytes accessed | tf_op | source)
XLA Modules:
  0.0 96.1 jit_solution(4282256653349947061)
XLA Ops:
  7.2 0.0 all-gather.3.cloned.1.call-start
  7.2 0.9 sine_bitcast_fusion
  8.1 1.4 %pad_maximum_fusion = f32[6,1,16,256]{3,2,1,0:T(8,128)} fusion(f32[1,1,16,256]{3,2,1,0:T(8,128)S(1)} %get-tuple-element.19, f32[1,1,16,256]{3,2,1,0:T(8,128)S(1)} %get-tuple-element.20, f32[1,1,16,256]{3,2,1,0:T(8,128)S(1)} %get-tuple-element.18, f32[3,1,16,256]{3,2,1,0:T(8,128)} %param.9), kind=kLoop, calls=%fused_computation | loop fusion | flops 73728 | bytes 196608 | tf_op jit(solution)/shard_map/concatenate | solution.py:645
  9.6 0.0 all-gather.3.cloned.1.call-update
  9.6 69.8 %excite.1 = (f32[4,4,64,1024]{3,2,1,0:T(8,128)}, f32[2,32,512]{2,1,0:T(8,128)}, f32[9,2,16,256]{3,2,1,0:T(8,128)}) custom-call(f32[4,4,64,1024]{3,2,1,0:T(8,128)} %states.1, f32[6,1,16,256]{3,2,1,0:T(8,128)} %cond_hbm.1, f32[2,32,512]{2,1,0:T(8,128)} %ten_hbm.1), custom_call_target="tpu_custom_call" | custom-call | flops 200000000 | bytes 16777216 | tf_op jit(solution)/shard_map/excite/pallas_call | solution.py:415
  79.4 0.6 pad_add_fusion.where
  80.0 0.0 all-gather.3.cloned.1.call-done
  80.0 9.2 %mechanics.1 = (f32[3,1,16,256]{3,2,1,0:T(8,128)}, f32[6,1,16,256]{3,2,1,0:T(8,128)}, f32[2,32,512]{2,1,0:T(8,128)}, f32[4,4,64,1024]{3,2,1,0:T(8,128)}) custom-call(s32[2]{0:T(128)} %pad_add_fusion.where, f32[16,6,16,256]{3,2,1,0:T(8,128)} %bitcast.9, f32[9,2,16,256]{3,2,1,0:T(8,128)} %get-tuple-element.11.active, f32[2,32,512]{2,1,0:T(8,128)} %get-tuple-element.12.ten_in, ...), custom_call_target="tpu_custom_call" | custom-call | tf_op jit(solution)/shard_map/mechanics/pallas_call | solution.py:614
Async XLA Ops:
  7.2 72.9 %all-gather.3.cloned.1.call-start = ((), (), s32[]{:S(2)}) async-start(), calls=%async_computation | async-start | bytes 1671168 | tf_op jit(solution)/shard_map/all_gather | solution.py:646
Sparse Core Ops, SparseCore 0:
  10.9 54.2 all-gather.2

commit v4 on v3

--- a/solution.py
+++ b/solution.py
@@ -59,9 +59,9 @@
 
 
 def excite_kernel(
-    slabs, states, cond_hbm, ten_hbm, out_hbm, ten_out, act_out,
+    slabs, states, cond_hbm, ten_hbm, fix_hbm, out_hbm, ten_out, act_out, fix_out,
     ubuf, out, cond, tension, coeff, dif, act_win,
-    load_sem, store_sem, sz, rz, sc, rc, sy, ry, sa, ra,
+    fix_win, load_sem, store_sem, sz, rz, sc, rc, sy, ry, sa, ra, sf, rf,
 ):
     grp = lax.axis_index("grp")
     slab = lax.axis_index("slab")
@@ -86,6 +86,8 @@
     load_c.start()
     load_g.start()
     load_t.start()
+    load_f = pltpu.make_async_copy(fix_hbm, fix_win.at[RADIUS, col], load_sem.at[4])
+    load_f.start()
 
     barrier = pltpu.get_barrier_semaphore()
 
@@ -93,7 +95,7 @@
         pl.semaphore_signal(barrier, inc=1, device_id=where, device_id_type=MESH)
 
     peers = -1
-    for d in range(-REACH, REACH + 1):
+    for d in range(-RADIUS, RADIUS + 1):
         valid = (slab + d >= 0) & (slab + d < slabs)
         peers = peers + 2 * valid.astype(jnp.int32)
 
@@ -105,7 +107,9 @@
 
         @pl.when(jnp.logical_not(valid))
         def _(d=d):
-            act_win[d + REACH] = jnp.zeros(act_win.shape[1:], F32)
+            fix_win[d + RADIUS, col] = jnp.zeros(fix_win.shape[2:], F32)
+            if abs(d) <= REACH:
+                act_win[d + REACH] = jnp.zeros(act_win.shape[1:], F32)
 
     blank = jnp.zeros((TILE, width), F32)
 
@@ -212,6 +216,44 @@
 
     load_g.wait()
     load_t.wait()
+
+    def copy_f(d):
+        return pltpu.make_async_remote_copy(
+            src_ref=fix_win.at[RADIUS, col],
+            dst_ref=fix_win.at[RADIUS - d, col],
+            send_sem=sf.at[d + RADIUS],
+            recv_sem=rf.at[RADIUS - d],
+            device_id=(grp, slab + d, col),
+            device_id_type=MESH,
+        )
+
+    def come_f(d):
+        return pltpu.make_async_remote_copy(
+            src_ref=fix_win.at[RADIUS, col],
+            dst_ref=fix_win.at[RADIUS + d, col],
+            send_sem=sf.at[d + RADIUS],
+            recv_sem=rf.at[RADIUS + d],
+            device_id=(grp, slab + d, col),
+            device_id_type=MESH,
+        )
+
+    def share_f(whose):
+        return pltpu.make_async_remote_copy(
+            src_ref=fix_win.at[:, whose],
+            dst_ref=fix_win.at[:, whose],
+            send_sem=sf.at[RADIUS],
+            recv_sem=rf.at[RADIUS],
+            device_id=(grp, slab, other),
+            device_id_type=MESH,
+        )
+
+    def each_f(act):
+        for d in range(-RADIUS, RADIUS + 1):
+            if d != 0:
+                pl.when((slab + d >= 0) & (slab + d < slabs))(lambda d=d: act(d))
+
+    load_f.wait()
+    each_f(lambda d: copy_f(d).start())
 
     lane = iota2((TILE, width), 1)
 
@@ -291,6 +333,11 @@
         step = n % tiles
         r = row_of(step)
 
+        @pl.when(n == 2 * tiles)
+        def _():
+            each_f(lambda d: come_f(d).wait_recv())
+            share_f(col).start()
+
         @pl.when(step == 0)
         def _():
             recv_z(k, 0)
@@ -374,6 +421,15 @@
                     act(d, col)
 
     each_a(lambda d, to: copy_a(d, to).start())
+    share_f(col).wait_send()
+    share_f(other).wait_recv()
+    each_f(lambda d: copy_f(d).wait_send())
+
+    def show(j, c):
+        fix_out[j] = fix_win[j]
+        return c
+
+    lax.fori_loop(0, 2 * RADIUS + 1, show, 0)
 
     copy_y(0).wait_send()
 
@@ -405,12 +461,13 @@
     act_out[...] = act_win[...]
 
 
-def excite(slabs, states, cond, tension):
+def excite(slabs, states, cond, tension, fixed):
     _, depth, rows, width = states.shape
     tiles = rows // TILE
     vmem = pl.BlockSpec(memory_space=pltpu.VMEM)
     hbm = pl.BlockSpec(memory_space=pltpu.HBM)
     window = (2 * REACH + 1, 2, *cond.shape[2:])
+    broad = (2 * RADIUS + 1, 2, *fixed.shape)
     dma = pltpu.SemaphoreType.DMA
     return pl.pallas_call(
         functools.partial(excite_kernel, slabs),
@@ -418,9 +475,10 @@
             jax.ShapeDtypeStruct(states.shape, F32),
             jax.ShapeDtypeStruct(tension.shape, F32),
             jax.ShapeDtypeStruct(window, F32),
+            jax.ShapeDtypeStruct(broad, F32),
         ),
-        in_specs=[hbm, hbm, hbm],
-        out_specs=(hbm, vmem, vmem),
+        in_specs=[hbm, hbm, hbm, hbm],
+        out_specs=(hbm, vmem, vmem, vmem),
         scratch_shapes=[
             pltpu.VMEM((SUB + 1, depth + 2, rows + 2 * TILE, width), F32),
             pltpu.VMEM(states.shape, F32),
@@ -429,7 +487,8 @@
             pltpu.VMEM((6, rows, width), F32),
             pltpu.VMEM((TILE, width), F32),
             pltpu.VMEM(window, F32),
-            dma((4,)),
+            pltpu.VMEM(broad, F32),
+            dma((5,)),
             dma((tiles,)),
             dma((SUB, 2, tiles)),
             dma((SUB, 2, tiles)),
@@ -439,6 +498,8 @@
             dma((SUB,)),
             dma((2 * REACH + 1, 2)),
             dma((2 * REACH + 1, 2)),
+            dma((2 * RADIUS + 1,)),
+            dma((2 * RADIUS + 1,)),
         ],
         compiler_params=pltpu.CompilerParams(
             collective_id=0, has_side_effects=True, vmem_limit_bytes=61 << 20
@@ -447,7 +508,7 @@
             flops=200_000_000, bytes_accessed=16 << 20, transcendentals=6_000_000
         ),
         name="excite",
-    )(states, cond, tension)
+    )(states, cond, tension, fixed)
 
 
 def first_piola(f, active, fdir):
@@ -546,13 +607,13 @@
             jnp.concatenate([a[half - TILE :], b], axis=0),
         )
 
-    def joined(zz, n):
-        return beside(fixed[2 * zz, n], fixed[2 * zz + 1, n])
+    def joined(j, n):
+        return beside(fixed[j, 0, n], fixed[j, 1, n])
 
     def fill(j, c):
         ok, zz = inside(j)
         for i in range(3):
-            win[i, j] = jnp.where(ok, joined(zz, i), 0.0)
+            win[i, j] = jnp.where(ok, joined(j, i), 0.0)
         return c
 
     lax.fori_loop(0, 2 * RADIUS + 1, fill, 0)
@@ -567,13 +628,31 @@
             f[i][i] = f[i][i] + 1.0
         return f
 
-    def directions(zz):
-        return [joined(zz, 3 + a) for a in range(3)]
+    def sine(x):
+        y = x * x
+        c = 1.0
+        for n in (12, 10, 8, 6, 4, 2):
+            c = 1.0 - y * (1.0 / (n * (n + 1))) * c
+        return x * c
+
+    def cosine(x):
+        y = x * x
+        c = 1.0
+        for n in (13, 11, 9, 7, 5, 3, 1):
+            c = 1.0 - y * (1.0 / (n * (n + 1))) * c
+        return c
+
+    def directions(j):
+        index = joined(j, 3)
+        theta = -1.0 + index * (2.0 / (NFIB - 1))
+        tilt = 0.3 * jnp.sin(3.0 * index)
+        flat = cosine(tilt)
+        return [sine(tilt), flat * sine(theta), flat * cosine(theta)]
 
     def stresses(j, c):
         ok, zz = inside(j)
         act = beside(active[j - 1, 0], active[j - 1, 1])
-        pieces = first_piola(deformation(j), act, directions(zz))
+        pieces = first_piola(deformation(j), act, directions(j))
         for n in range(9):
             stress[n, j] = jnp.where(ok, pieces[n], 0.0)
         return c
@@ -597,7 +676,7 @@
         reach = reach - 1
         lax.fori_loop(RADIUS - reach, RADIUS + reach + 1, move, 0)
 
-    comps = metric(deformation(RADIUS), directions(slab))
+    comps = metric(deformation(RADIUS), directions(RADIUS))
     for i in range(3):
         whole = win[i, RADIUS]
         disp_out[i, 0] = jnp.where(first, whole[:half], whole[TILE:])
@@ -632,19 +711,9 @@
     )(where, fixed, active, tension, states)
 
 
-def fiber_dir(fiber):
-    index = fiber.astype(F32)
-    theta = -1.0 + 2.0 * index / (NFIB - 1)
-    tilt = 0.3 * jnp.sin(3.0 * index)
-    return jnp.stack(
-        [jnp.sin(tilt), jnp.cos(tilt) * jnp.sin(theta), jnp.cos(tilt) * jnp.cos(theta)]
-    )
-
-
 def on_device(slabs, states, cond, tension, fiber, disp):
-    fixed = jnp.concatenate([disp, fiber_dir(fiber)])
-    fixed = lax.all_gather(fixed[:, 0], ("slab", "col"))
-    states_next, tension_next, active = excite(slabs, states, cond, tension)
+    fixed = jnp.concatenate([disp[:, 0], fiber.astype(F32)])
+    states_next, tension_next, active, fixed = excite(slabs, states, cond, tension, fixed)
     where = jnp.stack([lax.axis_index("slab"), lax.axis_index("col")]).astype(jnp.int32)
     disp_next, cond_next, tension_next, states_next = mechanics(
         slabs, where, fixed, active, tension_next, states_next

time: 96.3 us -> 87 us (0.903)
  between operations: 14.1 us -> 0.64 us
  Pallas kernels: 79 us -> 83.4 us
    pallas_call x1, Pallas kernels: 69.8 us -> 72.2 us  [excite(): pl.pallas_call(functools.partial(excite_kernel, slabs), out_shape=(jax.Sh...]
    pallas_call x1, Pallas kernels: 9.19 us -> 11.2 us  [mechanics(): pl.pallas_call(functools.partial(mech_kernel, slabs), out_shape=(jax.Shap...]
  transfers between devices with their start and end apart: 1 -> 0, of which waited for: 0 -> 0; matrix products, arithmetic and copies ran while one was open for 1% -> 0% of each run, Pallas kernels for 73% -> 0%
where the time goes in v4:
time: 87 us; the launch traced here: 86.8 us
  Pallas kernels  83.4 us (96%)
  other arithmetic  2.75 us (3%)
    pallas_call x1, Pallas kernels, excite(): pl.pallas_call(functools.partial(excite_kernel, slabs), out_shape=(jax.Sh...  72.2 us
    pallas_call x1, Pallas kernels, mechanics(): pl.pallas_call(functools.partial(mech_kernel, slabs), out_shape=(jax.Shap...  11.2 us

profile of v4, /device:TPU:0, one launch (start us, length us, event | category | flops | bytes accessed | tf_op | source)
XLA Modules:
  0.0 86.8 jit_solution(16640377665885455572)
XLA Ops:
  0.6 0.6 pad_add_fusion.where
  1.2 0.7 convert_element_type.3
  2.0 1.4 %pad_maximum_fusion.fix_hbm = f32[4,16,256]{2,1,0:T(8,128)} fusion(f32[1,16,256]{2,1,0:T(8,128)S(1)} %convert_element_type.3, f32[3,16,256]{2,1,0:T(8,128)} %bitcast.3), kind=kLoop, calls=%fused_computation | loop fusion | flops 16384 | bytes 131072 | tf_op jit(solution)/shard_map/concatenate | solution.py:715
  3.4 72.2 %excite.1 = (f32[4,4,64,1024]{3,2,1,0:T(8,128)}, f32[2,32,512]{2,1,0:T(8,128)}, f32[9,2,16,256]{3,2,1,0:T(8,128)}, f32[11,2,4,16,256]{4,3,2,1,0:T(8,128)}) custom-call(f32[4,4,64,1024]{3,2,1,0:T(8,128)} %states.1, f32[6,1,16,256]{3,2,1,0:T(8,128)} %cond_hbm.1, f32[2,32,512]{2,1,0:T(8,128)} %ten_hbm.1, f32[4,16,256]{2,1,0:T(8,128)} %pad_maximum_fusion.fix_hbm), custom_call_target="tpu_custom_call" | custom-call | flops 200000000 | bytes 16777216 | tf_op jit(solution)/shard_map/excite/pallas_call | solution.py:472
  75.6 11.2 %mechanics.1 = (f32[3,1,16,256]{3,2,1,0:T(8,128)}, f32[6,1,16,256]{3,2,1,0:T(8,128)}, f32[2,32,512]{2,1,0:T(8,128)}, f32[4,4,64,1024]{3,2,1,0:T(8,128)}) custom-call(s32[2]{0:T(128)} %pad_add_fusion.where, f32[11,2,4,16,256]{4,3,2,1,0:T(8,128)} %get-tuple-element.12.fixed, f32[9,2,16,256]{3,2,1,0:T(8,128)} %get-tuple-element.13.active, ...), custom_call_target="tpu_custom_call" | custom-call | tf_op jit(solution)/shard_map/mechanics/pallas_call | solution.py:693
